TPU v7x, 256 devices: a whole 4x4x8 slice. The times are simulated.
256 devices in a mesh: movie: 128 (over z, y, x), user: 2 (over core).
Axes of the slice: x: 4, y: 4, z: 8, core: 2. Of those that a mesh axis runs over, the one named last changes fastest.
Arguments:
- movie_ids: int32 [1024, 128], P(('movie', 'user')), may hold values from 0 to 17919, as said below
- ratings: int32 [1024, 128], P(('movie', 'user')), may hold values from 0 to 4
- valid: int32 [1024, 128], P(('movie', 'user')), may hold values from 0 to 1, as said below
- weights: bfloat16 [5, 17920, 1024], P(None, 'movie'), may hold values from -0.5 to 0.5
- vis_bias: float32 [5, 17920], P(None, 'movie'), may hold values from -5 to 260
- hid_bias: float32 [1024], replicated, may hold values from -5 to 5
Outputs:
- weight_grad: float32 [5, 17920, 1024], P(None, 'movie')
- visible_grad: float32 [5, 17920], P(None, 'movie')
- hidden_grad: float32 [1024], replicated
- positive_hidden: float32 [1024, 1024], P(('movie', 'user'))
Inputs may be any that keep to these rules, and one draw needn't show every extreme that they name: `movie_ids`: movie ids within one user's block are distinct. Of the slots with valid 1 among the users of one device (4 consecutive users), at most 12 name movies of any one block of 140 consecutive movie ids; in every draw some such block takes exactly 12 from the users of every device. Slots with valid 0 are padding and count nowhere.
All inputs are finite; a program needn't handle non-finite values.
Results may differ from a plain program's by a relative error of at most 0.0054.
Values may be sent and summed in bfloat16 or wider, within the bound.
A program may use at most 64 MiB of HBM per device.

v0:
```python
import jax
import jax.numpy as jnp
from jax import lax
from jax.sharding import Mesh
from jax.sharding import PartitionSpec as P

MOVIE = ("movie_0", "movie_1", "movie_2")
MOVIE_USER = ("movie_0", "movie_1", "movie_2", "user")


def in_blocks(x, dim, devices):
    lengths = x.shape
    tiles = x.reshape(*lengths[:dim], devices, lengths[dim] // devices, *lengths[dim + 1 :])
    return jnp.moveaxis(tiles, dim, 0)


def summed_on_arrival(x, axis, dim):
    tiles = in_blocks(x, dim, lax.axis_size(axis))
    arrived = lax.all_to_all(tiles, axis, split_axis=0, concat_axis=0, tiled=True)
    return arrived.astype(jnp.float32).sum(axis=0)


def summed_rows(x, axes, dim):
    far, near = axes
    own = summed_on_arrival(in_blocks(x, dim, lax.axis_size(far)), near, dim + 1)
    return jnp.sum(
        lax.all_to_all(own.astype(jnp.bfloat16), far, 0, 0, tiled=True).astype(jnp.float32), axis=0
    )


def from_everyone(x, axis):
    devices = lax.axis_size(axis)
    return lax.all_to_all(jnp.broadcast_to(x[None], (devices, *x.shape)), axis, 0, 0, tiled=True)


def in_order(tiles, dim):
    tiles = jnp.moveaxis(tiles, 0, dim)
    lengths = tiles.shape
    return tiles.reshape(*lengths[:dim], lengths[dim] * lengths[dim + 1], *lengths[dim + 2 :])


def gather_axes(x, axes, dim):
    far, near = axes
    leading = from_everyone(x, far)
    tiles = jnp.swapaxes(from_everyone(leading, near), 0, 1)
    return in_order(tiles.reshape(-1, *x.shape), dim)


def side_by_side(arrays, axis, split_dim, concat_dim, along):
    both = jnp.concatenate(arrays, axis=along)
    out, at, finished = (
        lax.all_to_all(both, axis, split_axis=split_dim, concat_axis=concat_dim, tiled=True),
        0,
        [],
    )
    for a in arrays:
        finished.append(lax.slice_in_dim(out, at, at + a.shape[along], axis=along))
        at += a.shape[along]
    return tuple(finished)


def taken_together(x, axis):
    everything = from_everyone(x, axis)
    return jnp.sum(everything.astype(jnp.float32), axis=0)


def taken_together_2(x, axis):
    everything = from_everyone(x, axis)
    return jnp.sum(everything, axis=0)


def one_axis_at_a_time(x, axes):
    far, near = axes
    return taken_together_2(taken_together_2(x, near), far)


def reconstruct(hidden_rows, weight_table, bias_row, rated_mask, levels):
    group_rows = hidden_rows.shape[0]
    rating_logits = (
        lax.dot_general(
            hidden_rows, weight_table, (((1,), (1,)), ((), ())), preferred_element_type=jnp.float32
        )
        + bias_row[None, :]
    )
    shaped = rating_logits.reshape(group_rows, levels, -1)
    largest = jnp.max(shaped, axis=1, keepdims=True)
    exponent = jnp.exp(shaped - largest)
    softened = (exponent / jnp.sum(exponent, axis=1, keepdims=True)).astype(jnp.bfloat16)
    return (softened * rated_mask[:, None, :]).reshape(group_rows, -1)


def hidden_phase(visible, weight_table, hid_bias):
    summed = summed_rows(
        jnp.dot(visible, weight_table, preferred_element_type=jnp.float32).astype(jnp.bfloat16),
        ("movie_0", ("movie_1", "movie_2")),
        0,
    )
    own_rows = jax.nn.sigmoid(hid_bias[None, :] + summed)
    shared = gather_axes(own_rows.astype(jnp.bfloat16), (("movie_0", "movie_1"), "movie_2"), 0)
    return (own_rows, shared)


def on_device(movie_ids, ratings, valid, weights, vis_bias, hid_bias):
    owners = lax.axis_size(MOVIE)
    local_users, slot_count = movie_ids.shape
    levels, local_movies, hidden = weights.shape
    columns = levels * local_movies
    group_rows = owners * local_users
    capacity = max(2, 3 * local_users * slot_count // owners)
    flat_ids = movie_ids.reshape(-1)
    owner_ids = flat_ids // local_movies
    column_ids = ratings.reshape(-1) * local_movies + flat_ids % local_movies
    user_ids = jnp.arange(local_users * slot_count, dtype=jnp.int32) // slot_count
    usable = valid.reshape(-1) == 1
    matches = (owner_ids[:, None] == jnp.arange(owners, dtype=jnp.int32)[None, :]) & usable[:, None]
    ranking = jnp.cumsum(matches.astype(jnp.int32), axis=0) - 1
    placed = jnp.sum(jnp.where(matches, ranking, 0), axis=1)
    target = jnp.where(usable, owner_ids, owners)
    user_slots = (
        jnp.zeros((owners, capacity), jnp.int32).at[target, placed].set(user_ids, mode="drop")
    )
    column_slots = (
        jnp.full((owners, capacity), -1, jnp.int32).at[target, placed].set(column_ids, mode="drop")
    )
    got_users, got_columns = side_by_side((user_slots, column_slots), MOVIE, 0, 0, 1)
    user_hot = (got_users[:, :, None] == jnp.arange(local_users, dtype=jnp.int32)).astype(
        jnp.bfloat16
    )
    column_hot = (got_columns[:, :, None] == jnp.arange(columns, dtype=jnp.int32)).astype(
        jnp.bfloat16
    )
    shown = jnp.einsum("ncu,ncj->nuj", user_hot, column_hot, preferred_element_type=jnp.float32)
    shown = shown.reshape(group_rows, columns).astype(jnp.bfloat16)
    rated_mask = jnp.sum(shown.reshape(group_rows, levels, local_movies), axis=1)
    weight_table = weights.reshape(columns, hidden)
    positive_own, positive_group = hidden_phase(shown, weight_table, hid_bias)
    reconstructed_ratings = reconstruct(
        positive_group, weight_table, vis_bias.reshape(columns), rated_mask, levels
    )
    negative_own, negative_group = hidden_phase(reconstructed_ratings, weight_table, hid_bias)
    contract = (((0,), (0,)), ((), ()))
    weight_grad = lax.dot_general(
        shown, positive_group, contract, preferred_element_type=jnp.float32
    )
    weight_grad = weight_grad - lax.dot_general(
        reconstructed_ratings, negative_group, contract, preferred_element_type=jnp.float32
    )
    visible_grad = jnp.sum(shown.astype(jnp.float32), axis=0) - jnp.sum(
        reconstructed_ratings.astype(jnp.float32), axis=0
    )
    weight_grad, visible_grad = (
        taken_together(weight_grad.astype(jnp.bfloat16), "user").astype(jnp.float32),
        taken_together(visible_grad.astype(jnp.bfloat16), "user").astype(jnp.float32),
    )
    hidden_grad = one_axis_at_a_time(
        jnp.sum(positive_own - negative_own, axis=0), (("movie_0", "movie_1"), ("movie_2", "user"))
    )
    return (
        weight_grad.reshape(levels, local_movies, hidden),
        visible_grad.reshape(levels, local_movies),
        hidden_grad,
        positive_own,
    )


def solution(mesh):
    split = Mesh(
        mesh.devices.reshape(8, 4, 4, mesh.shape["user"]), ("movie_0", "movie_1", "movie_2", "user")
    )
    in_specs = (
        P(MOVIE_USER, None),
        P(MOVIE_USER, None),
        P(MOVIE_USER, None),
        P(None, MOVIE, None),
        P(None, MOVIE),
        P(),
    )
    out_specs = (P(None, MOVIE, None), P(None, MOVIE), P(), P(MOVIE_USER, None))
    return jax.shard_map(
        on_device, mesh=split, in_specs=in_specs, out_specs=out_specs, check_vma=False
    )
```

profile of v0, /device:TPU:1, one launch (start us, length us, event | category | flops | bytes accessed | tf_op | source)
XLA Modules:
  0.0 271.9 jit_solution(2248238722709036509)
XLA Ops:
  4.5 24.6 %scatter_fusion.1 = s32[128,12]{0,1:T(8,128)S(1)} fusion(s32[128,12]{0,1:T(8,128)S(1)} %broadcast_in_dim.31, s32[512]{0:T(512)S(1)} %bitcast.78, s32[512]{0:T(512)S(1)} %get-tuple-element.14), kind=kCustom, calls=%fused_computation.1 | custom fusion | bytes 10240 | tf_op jit(solution)/shard_map/scatter | solution.py:123
  29.2 24.6 %scatter_fusion = s32[128,12]{0,1:T(8,128)S(1)} fusion(s32[128,12]{0,1:T(8,128)S(1)} %broadcast_in_dim.28, s32[512]{0:T(512)S(1)} %bitcast.79, s32[512]{0:T(512)S(1)} %add_select_fusion.1), kind=kCustom, calls=%fused_computation | custom fusion | bytes 10240 | tf_op jit(solution)/shard_map/scatter | solution.py:120
  54.5 16.3 %all-to-all-start = ((s32[128,1,24]{2,1,0:T(1,128)}), s32[128,1,24]{2,1,0:T(1,128)S(1)}, u32[]{:S(2)}, u32[]{:S(2)}) async-start(s32[128,1,24]{2,1,0:T(1,128)} %copy.55), calls=%async_computation | async-start | bytes 131072 | tf_op jit(solution)/shard_map/all_to_all | solution.py:52
  71.1 10.5 %all-to-all-done = s32[128,1,24]{2,1,0:T(1,128)S(1)} async-done(((s32[128,1,24]{2,1,0:T(1,128)}), s32[128,1,24]{2,1,0:T(1,128)S(1)}, u32[]{:S(2)}, u32[]{:S(2)}) %all-to-all-start) | async-done | bytes 12320 | tf_op jit(solution)/shard_map/all_to_all | solution.py:52
  88.3 18.0 %all_to_all.75 = bf16[16,8,4,1024]{3,2,1,0:T(4,128)(2,1)S(1)} all-to-all(bf16[16,8,4,1024]{3,2,1,0:T(4,128)(2,1)S(1)} %bitcast.81), channel_id=1, replica_groups=mesh['movie_0'=8,'movie_1'=4,'movie_2'=4,'user'=2] {'movie_1','movie_2'}, dimensions={0} | all-to-all | bytes 2097152 | tf_op jit(solution)/shard_map/all_to_all | solution.py:19
  106.8 9.6 %all_to_all.76 = bf16[8,4,1024]{2,1,0:T(4,128)(2,1)S(1)} all-to-all(bf16[8,4,1024]{2,1,0:T(4,128)(2,1)S(1)} %reduce_sum.139), channel_id=1, replica_groups=mesh['movie_0'=8,'movie_1'=4,'movie_2'=4,'user'=2] {'movie_0'}, dimensions={0} | all-to-all | bytes 131072 | tf_op jit(solution)/shard_map/all_to_all | solution.py:27
  116.6 13.6 %all_to_all.77 = bf16[32,4,1024]{2,1,0:T(4,128)(2,1)S(1)} all-to-all(bf16[32,4,1024]{2,1,0:T(4,128)(2,1)S(1)} %broadcast_in_dim.32), channel_id=1, replica_groups=mesh['movie_0'=8,'movie_1'=4,'movie_2'=4,'user'=2] {'movie_0','movie_1'}, dimensions={0} | all-to-all | bytes 524288 | tf_op jit(solution)/shard_map/all_to_all | solution.py:33
  131.5 3.7 %all-to-all-start.4 = ((bf16[4,32,4,1024]{3,2,1,0:T(4,128)(2,1)}), bf16[4,32,4,1024]{3,2,1,0:T(4,128)(2,1)S(1)}, u32[]{:S(2)}, u32[]{:S(2)}) async-start(bf16[4,32,4,1024]{3,2,1,0:T(4,128)(2,1)} %broadcast_in_dim.33), calls=%async_computation.4 | async-start | bytes 2097152 | tf_op jit(solution)/shard_map/all_to_all | solution.py:33
  135.3 3.3 %convert_element_type.88 = bf16[512,5,140]{2,1,0:T(8,128)(2,1)S(1)} reshape(bf16[128,4,700]{2,1,0:T(4,128)(2,1)} %copy-done.2) | data formatting | bytes 1433600 | tf_op jit(solution)/shard_map/convert_element_type | solution.py:133
  140.8 3.9 %all-to-all-done.4 = bf16[4,32,4,1024]{3,2,1,0:T(4,128)(2,1)S(1)} async-done(((bf16[4,32,4,1024]{3,2,1,0:T(4,128)(2,1)}), bf16[4,32,4,1024]{3,2,1,0:T(4,128)(2,1)S(1)}, u32[]{:S(2)}, u32[]{:S(2)}) %all-to-all-start.4) | async-done | bytes 1048608 | tf_op jit(solution)/shard_map/all_to_all | solution.py:33
  155.7 4.5 %all-to-all-start.5 = ((bf16[16,8,4,1024]{3,2,1,0:T(4,128)(2,1)}), bf16[16,8,4,1024]{3,2,1,0:T(4,128)(2,1)}, u32[]{:S(2)}, u32[]{:S(2)}) async-start(bf16[16,8,4,1024]{3,2,1,0:T(4,128)(2,1)} %bitcast.76), calls=%async_computation.5 | async-start | bytes 2097152 | tf_op jit(solution)/shard_map/all_to_all | solution.py:19
  164.1 8.6 %all-to-all-done.5 = bf16[16,8,4,1024]{3,2,1,0:T(4,128)(2,1)} async-done(((bf16[16,8,4,1024]{3,2,1,0:T(4,128)(2,1)}), bf16[16,8,4,1024]{3,2,1,0:T(4,128)(2,1)}, u32[]{:S(2)}, u32[]{:S(2)}) %all-to-all-start.5) | async-done | bytes 1048608 | tf_op jit(solution)/shard_map/all_to_all | solution.py:19
  175.0 3.3 %all-to-all-start.6 = ((bf16[8,4,1024]{2,1,0:T(4,128)(2,1)}), bf16[8,4,1024]{2,1,0:T(4,128)(2,1)S(1)}, u32[]{:S(2)}, u32[]{:S(2)}) async-start(bf16[8,4,1024]{2,1,0:T(4,128)(2,1)} %reduce_sum.143), calls=%async_computation.6 | async-start | bytes 131072 | tf_op jit(solution)/shard_map/all_to_all | solution.py:27
  178.4 3.1 %convert_reduce_fusion.2 = (f32[700]{0:T(1024)S(1)}, bf16[512,700]{0,1:T(8,128)(2,1)}) fusion(bf16[512,700]{0,1:T(8,128)(2,1)S(1)} %copy-done.3, f32[512,700]{0,1:T(8,128)} %div.63, f32[512,700]{0,1:T(8,128)S(1)} %convolution_add_fusion, f32[512,700]{0,1:T(8,128)} %sub.56), kind=kLoop, calls=%fused_computation.13 | loop fusion | flops 2149700 | bytes 5737200 | tf_op jit(solution)/shard_map/reduce_sum | solution.py:148
  181.5 4.0 %all-to-all-done.6 = bf16[8,4,1024]{2,1,0:T(4,128)(2,1)S(1)} async-done(((bf16[8,4,1024]{2,1,0:T(4,128)(2,1)}), bf16[8,4,1024]{2,1,0:T(4,128)(2,1)S(1)}, u32[]{:S(2)}, u32[]{:S(2)}) %all-to-all-start.6) | async-done | bytes 65568 | tf_op jit(solution)/shard_map/all_to_all | solution.py:27
  186.3 11.4 %all-to-all-start.11 = ((f32[8,1,1024]{2,1,0:T(1,128)}), f32[8,1,1024]{2,1,0:T(1,128)S(1)}, u32[]{:S(2)}, u32[]{:S(2)}) async-start(f32[8,1,1024]{2,1,0:T(1,128)} %broadcast_in_dim.38), calls=%async_computation.11 | async-start | bytes 65536 | tf_op jit(solution)/shard_map/all_to_all | solution.py:33
  199.6 2.9 %all-to-all-done.11 = f32[8,1,1024]{2,1,0:T(1,128)S(1)} async-done(((f32[8,1,1024]{2,1,0:T(1,128)}), f32[8,1,1024]{2,1,0:T(1,128)S(1)}, u32[]{:S(2)}, u32[]{:S(2)}) %all-to-all-start.11) | async-done | bytes 32800 | tf_op jit(solution)/shard_map/all_to_all | solution.py:33
  202.5 3.9 %all-to-all-start.10 = ((bf16[2,2,350]{2,1,0:T(2,128)(2,1)}), bf16[2,2,350]{2,1,0:T(2,128)(2,1)S(1)}, u32[]{:S(2)}, u32[]{:S(2)}) async-start(bf16[2,2,350]{2,1,0:T(2,128)(2,1)} %reshape.265), calls=%async_computation.10 | async-start | bytes 6144 | tf_op jit(solution)/shard_map/all_to_all | solution.py:33
  207.5 12.9 %all_to_all.78 = f32[32,1,1024]{2,1,0:T(1,128)S(1)} all-to-all(f32[32,1,1024]{2,1,0:T(1,128)S(1)} %broadcast_in_dim.39), channel_id=1, replica_groups=mesh['movie_0'=8,'movie_1'=4,'movie_2'=4,'user'=2] {'movie_0','movie_1'}, dimensions={0} | all-to-all | bytes 262144 | tf_op jit(solution)/shard_map/all_to_all | solution.py:33
  220.4 13.9 %all_to_all.79 = bf16[32,4,1024]{2,1,0:T(4,128)(2,1)S(1)} all-to-all(bf16[32,4,1024]{2,1,0:T(4,128)(2,1)S(1)} %broadcast_in_dim.34), channel_id=1, replica_groups=mesh['movie_0'=8,'movie_1'=4,'movie_2'=4,'user'=2] {'movie_0','movie_1'}, dimensions={0} | all-to-all | bytes 524288 | tf_op jit(solution)/shard_map/all_to_all | solution.py:33
  235.6 4.5 %all-to-all-start.8 = ((bf16[4,32,4,1024]{3,2,1,0:T(4,128)(2,1)}), bf16[4,32,4,1024]{3,2,1,0:T(4,128)(2,1)}, u32[]{:S(2)}, u32[]{:S(2)}) async-start(bf16[4,32,4,1024]{3,2,1,0:T(4,128)(2,1)} %broadcast_in_dim.35), calls=%async_computation.8 | async-start | bytes 2097152 | tf_op jit(solution)/shard_map/all_to_all | solution.py:33
  243.9 7.5 %all-to-all-done.8 = bf16[4,32,4,1024]{3,2,1,0:T(4,128)(2,1)} async-done(((bf16[4,32,4,1024]{3,2,1,0:T(4,128)(2,1)}), bf16[4,32,4,1024]{3,2,1,0:T(4,128)(2,1)}, u32[]{:S(2)}, u32[]{:S(2)}) %all-to-all-start.8) | async-done | bytes 1048608 | tf_op jit(solution)/shard_map/all_to_all | solution.py:33
  251.4 2.8 %copy.62 = bf16[32,4,4,1024]{3,2,1,0:T(4,128)(2,1)} copy(bf16[32,4,4,1024]{3,2,0,1:T(4,128)(2,1)} %bitcast.17) | data formatting | bytes 2097152 | tf_op jit(solution)/shard_map/transpose | solution.py:45
  259.1 10.2 %all_to_all.80 = bf16[2,700,1024]{2,1,0:T(8,128)(2,1)S(1)} all-to-all(bf16[2,700,1024]{2,1,0:T(8,128)(2,1)S(1)} %broadcast_in_dim.36), channel_id=1, replica_groups=mesh['movie_0'=8,'movie_1'=4,'movie_2'=4,'user'=2] {'user'}, dimensions={0} | all-to-all | bytes 5734400 | tf_op jit(solution)/shard_map/all_to_all | solution.py:33
  (102 shorter events, 49.2 us)
Async XLA Ops:
  0.6 3.5 %copy-start.12 = (s32[4,128]{1,0:T(4,128)S(1)}, s32[4,128]{1,0:T(4,128)}, u32[]{:S(2)}) copy-start(s32[4,128]{1,0:T(4,128)} %param.6) | copy-start | bytes 6148
  0.6 3.5 %copy-start.13 = (s32[4,128]{1,0:T(4,128)S(1)}, s32[4,128]{1,0:T(4,128)}, u32[]{:S(2)}) copy-start(s32[4,128]{1,0:T(4,128)} %param.7) | copy-start | bytes 6148
  29.2 41.7 %copy-start.4 = (bf16[5,140,1024]{2,1,0:T(8,128)(2,1)S(1)}, bf16[5,140,1024]{2,1,0:T(8,128)(2,1)}, u32[]{:S(2)}) copy-start(bf16[5,140,1024]{2,1,0:T(8,128)(2,1)} %param.9) | copy-start | bytes 4300804
  54.5 27.1 %all-to-all-start = ((s32[128,1,24]{2,1,0:T(1,128)}), s32[128,1,24]{2,1,0:T(1,128)S(1)}, u32[]{:S(2)}, u32[]{:S(2)}) async-start(s32[128,1,24]{2,1,0:T(1,128)} %copy.55), calls=%async_computation | async-start | bytes 131072 | tf_op jit(solution)/shard_map/all_to_all | solution.py:52
  71.1 12.7 %copy-start.6 = (bf16[700,1024]{1,0:T(8,128)(2,1)}, bf16[700,1024]{1,0:T(8,128)(2,1)S(1)}, u32[]{:S(2)}) copy-start(bf16[700,1024]{1,0:T(8,128)(2,1)S(1)} %reshape.248) | copy-start | bytes 4300804
  83.4 0.9 copy-start.2
  84.3 2.0 copy-start
  88.3 28.2 %copy-start.10 = (f32[1024]{0:T(1024)S(1)}, f32[1024]{0:T(1024)}, u32[]{:S(2)}) copy-start(f32[1024]{0:T(1024)} %param.11) | copy-start | bytes 12292
  116.5 69.1 %copy-start.9 = (f32[4,1024]{1,0:T(4,128)}, f32[4,1024]{1,0:T(4,128)S(1)}, u32[]{:S(2)}) copy-start(f32[4,1024]{1,0:T(4,128)S(1)} %get-tuple-element.9) | copy-start | bytes 49156
  130.2 5.0 %copy-start.11 = (f32[5,140]{1,0:T(8,128)S(1)}, f32[5,140]{1,0:T(8,128)}, u32[]{:S(2)}) copy-start(f32[5,140]{1,0:T(8,128)} %param.10) | copy-start | bytes 8404
  131.5 13.3 %all-to-all-start.4 = ((bf16[4,32,4,1024]{3,2,1,0:T(4,128)(2,1)}), bf16[4,32,4,1024]{3,2,1,0:T(4,128)(2,1)S(1)}, u32[]{:S(2)}, u32[]{:S(2)}) async-start(bf16[4,32,4,1024]{3,2,1,0:T(4,128)(2,1)} %broadcast_in_dim.33), calls=%async_computation.4 | async-start | bytes 2097152 | tf_op jit(solution)/shard_map/all_to_all | solution.py:33
  145.6 1.0 copy-start.1
  149.2 1.4 copy-start.5
  149.2 1.4 copy-start.7
  155.7 4.5 %copy-start.8 = (bf16[512,140]{0,1:T(8,128)(2,1)S(1)}, bf16[512,140]{0,1:T(8,128)(2,1)}, u32[]{:S(2)}) copy-start(bf16[512,140]{0,1:T(8,128)(2,1)} %copy.59) | copy-start | bytes 430084
  155.7 17.1 %all-to-all-start.5 = ((bf16[16,8,4,1024]{3,2,1,0:T(4,128)(2,1)}), bf16[16,8,4,1024]{3,2,1,0:T(4,128)(2,1)}, u32[]{:S(2)}, u32[]{:S(2)}) async-start(bf16[16,8,4,1024]{3,2,1,0:T(4,128)(2,1)} %bitcast.76), calls=%async_computation.5 | async-start | bytes 2097152 | tf_op jit(solution)/shard_map/all_to_all | solution.py:19
  164.1 14.3 %copy-start.3 = (bf16[512,700]{0,1:T(8,128)(2,1)S(1)}, bf16[512,700]{0,1:T(8,128)(2,1)}, u32[]{:S(2)}) copy-start(bf16[512,700]{0,1:T(8,128)(2,1)} %mul.23) | copy-start | bytes 2150404
  175.0 10.5 %all-to-all-start.6 = ((bf16[8,4,1024]{2,1,0:T(4,128)(2,1)}), bf16[8,4,1024]{2,1,0:T(4,128)(2,1)S(1)}, u32[]{:S(2)}, u32[]{:S(2)}) async-start(bf16[8,4,1024]{2,1,0:T(4,128)(2,1)} %reduce_sum.143), calls=%async_computation.6 | async-start | bytes 131072 | tf_op jit(solution)/shard_map/all_to_all | solution.py:27
  186.3 16.2 %all-to-all-start.11 = ((f32[8,1,1024]{2,1,0:T(1,128)}), f32[8,1,1024]{2,1,0:T(1,128)S(1)}, u32[]{:S(2)}, u32[]{:S(2)}) async-start(f32[8,1,1024]{2,1,0:T(1,128)} %broadcast_in_dim.38), calls=%async_computation.11 | async-start | bytes 65536 | tf_op jit(solution)/shard_map/all_to_all | solution.py:33
  202.5 5.0 %all-to-all-start.10 = ((bf16[2,2,350]{2,1,0:T(2,128)(2,1)}), bf16[2,2,350]{2,1,0:T(2,128)(2,1)S(1)}, u32[]{:S(2)}, u32[]{:S(2)}) async-start(bf16[2,2,350]{2,1,0:T(2,128)(2,1)} %reshape.265), calls=%async_computation.10 | async-start | bytes 6144 | tf_op jit(solution)/shard_map/all_to_all | solution.py:33
  235.6 15.8 %all-to-all-start.8 = ((bf16[4,32,4,1024]{3,2,1,0:T(4,128)(2,1)}), bf16[4,32,4,1024]{3,2,1,0:T(4,128)(2,1)}, u32[]{:S(2)}, u32[]{:S(2)}) async-start(bf16[4,32,4,1024]{3,2,1,0:T(4,128)(2,1)} %broadcast_in_dim.35), calls=%async_computation.8 | async-start | bytes 2097152 | tf_op jit(solution)/shard_map/all_to_all | solution.py:33
where the time goes:
time: 273 us; the launch traced here: 272 us
  local copies, waits for them, and re-layouts  80.1 us (29%)
  blocking collectives  78.1 us (29%)
  starting transfers between devices  47.7 us (17%)
  waiting for transfers between devices  38.5 us (14%)
  other arithmetic  13.5 us (5%)
  matrix products  12.9 us (5%)
    all_to_all x4, blocking collectives, from_everyone(): lax.all_to_all(jnp.broadcast_to(x[None], (devices, *x.shape)), axis, 0, 0...  50.5 us
    scatter x1, local copies, waits for them, and re-layouts, on_device(): jnp.full((owners, capacity), -1, jnp.int32).at[target, placed]  24.6 us
    scatter x1, local copies, waits for them, and re-layouts, on_device(): jnp.zeros((owners, capacity), jnp.int32).at[target, placed]  24.6 us
    all_to_all x4, starting transfers between devices, from_everyone(): lax.all_to_all(jnp.broadcast_to(x[None], (devices, *x.shape)), axis, 0, 0...  23.5 us
    all_to_all x1, blocking collectives, summed_on_arrival(): lax.all_to_all(tiles, axis, split_axis=0, concat_axis=0, tiled=True)  18 us
    all_to_all x1, starting transfers between devices, side_by_side(): lax.all_to_all(both, axis, split_axis=split_dim, concat_axis=concat_dim,...  16.3 us
    all_to_all x4, waiting for transfers between devices, from_everyone(): lax.all_to_all(jnp.broadcast_to(x[None], (devices, *x.shape)), axis, 0, 0...  15.3 us
    all_to_all x1, waiting for transfers between devices, side_by_side(): lax.all_to_all(both, axis, split_axis=split_dim, concat_axis=concat_dim,...  10.5 us
  transfers between devices with their start and end apart: 7, of which 7 were waited for; matrix products, arithmetic and copies ran while one was open for 7% of the time, Pallas kernels for 0%

commit v1 on v0

v1 whole, which is shorter than its diff:
```python
import functools

import jax
import jax.numpy as jnp
from jax import lax
from jax.experimental import pallas as pl
from jax.experimental.pallas import tpu as pltpu
from jax.sharding import Mesh
from jax.sharding import PartitionSpec as P

LEVELS = 5
MOV = 140
PAD = 144
COLS = LEVELS * PAD
F = 1024
NZ, NXY = 8, 16
CAP = 12
USERS = 512
GROUPS = 2
U = USERS // GROUPS
R = U // NXY
ALL = ("z", "y", "x", "core")
MESH = pl.DeviceIdType.MESH
F32, BF16 = jnp.float32, jnp.bfloat16


def dot(a, b, ca, cb):
    return lax.dot_general(a, b, (((ca,), (cb,)), ((), ())), preferred_element_type=F32)


def kernel(
    ids_ref, rat_ref, val_ref, w_ref, vb_ref, hb_ref,
    wg_ref, vg_ref, hg_ref, ph_ref,
    w_sc, vb_pad, vbc, t2d, t_send, d1, d2, s_sc, r_sc, l_sc,
    p_sc, r1, q_sc, r2, hid, pos_own, acc_sc, own_sc, oth_sc,
    hz, hxy, hco, vco,
    dz_s, dz_r, dx_s, dx_r, cz_s, cz_r, cx_s, cx_r, hz_s, hz_r, hx_s, hx_r, co_s, co_r,
):
    z, y, x, core = [lax.axis_index(a) for a in ALL]
    xy = y * 4 + x
    other = (z, y, x, 1 - core)

    def xy_peer(d):
        return lax.rem(y + d // 4, 4), lax.rem(x + lax.rem(d, 4), 4)

    def z_peer(d):
        return lax.rem(z + d, NZ)

    def xy_copies(src, dst, send, recv):
        def copy(d):
            ty, tx = xy_peer(d)
            return pltpu.make_async_remote_copy(
                src(ty * 4 + tx), dst(d), send.at[d], recv.at[d],
                device_id=(z, ty, tx, core), device_id_type=MESH,
            )

        return NXY, copy

    def z_copies(src, dst, send, recv):
        def copy(d):
            tz = z_peer(d)
            return pltpu.make_async_remote_copy(
                src(tz), dst(d), send.at[d], recv.at[d],
                device_id=(tz, y, x, core), device_id_type=MESH,
            )

        return NZ, copy

    def each(copies, act):
        n, copy = copies

        def step(d, carry):
            act(copy(d))
            return carry

        lax.fori_loop(1, n, step, 0)

    def start(copies):
        each(copies, lambda c: c.start())

    def arrived(copies):
        each(copies, lambda c: c.wait_recv())

    def sent(copies):
        each(copies, lambda c: c.wait_send())

    barrier = pltpu.get_barrier_semaphore()

    def greet_xy(d, carry):
        ty, tx = xy_peer(d)
        pl.semaphore_signal(barrier, 1, device_id=(z, ty, tx, core), device_id_type=MESH)
        return carry

    def greet_z(d, carry):
        pl.semaphore_signal(barrier, 1, device_id=(z_peer(d), y, x, core), device_id_type=MESH)
        return carry

    lax.fori_loop(1, NZ, greet_z, 0)
    lax.fori_loop(1, NXY, greet_xy, 0)
    pl.semaphore_signal(barrier, 1, device_id=other, device_id_type=MESH)

    ids = ids_ref[...]
    owner = jnp.floor((ids.astype(F32) + 0.5) * (1.0 / MOV)).astype(jnp.int32)
    column = rat_ref[...] * PAD + (ids - owner * MOV) + 1
    high = lax.shift_right_logical(column, 5).astype(F32)
    low = (column & 31).astype(F32)
    owner = jnp.where(val_ref[...] == 1, owner, -1)
    row = lax.broadcasted_iota(jnp.int32, (128, 128), 0)
    lane = lax.broadcasted_iota(jnp.int32, (128, 128), 1)
    before = jnp.where(row < lane, 1.0, 0.0).astype(BF16)
    rank_row = (row & 15).astype(F32)
    user_row = lax.shift_right_logical(row, 4) & 3
    table = jnp.zeros((128, 128), F32)
    for u in range(4):
        hot = jnp.where(owner[u : u + 1] == row, 1.0, 0.0)
        hot_low = hot.astype(BF16)
        rank = jnp.sum(hot * dot(hot_low, before, 1, 0), axis=0, keepdims=True)
        part = jnp.where(row < 64, high[u : u + 1], low[u : u + 1])
        pick = jnp.where((user_row == u) & (rank_row == rank), part, 0.0)
        table = table + dot(hot_low, pick.astype(BF16), 1, 1)
    t2d[...] = table

    def spread(i, carry):
        t_send[i // NXY, lax.rem(i, NXY)] = t2d[pl.ds(i, 1), :]
        return carry

    lax.fori_loop(0, 128, spread, 0)

    for k in range(LEVELS):
        w_sc[k * PAD + 128 : (k + 1) * PAD] = jnp.zeros((PAD - 128, F), BF16)
        w_sc[k * PAD : k * PAD + MOV] = w_ref[k]
    vb_pad[...] = jnp.zeros((8, 256), F32)
    vb_pad[0:LEVELS, 0:MOV] = vb_ref[...]
    bias_columns = jnp.transpose(vb_pad[...])
    for k in range(LEVELS):
        vbc[k * PAD : (k + 1) * PAD] = jnp.broadcast_to(bias_columns[0:PAD, k : k + 1], (PAD, 128))

    pl.semaphore_wait(barrier, NZ - 1 + NXY - 1 + 1)

    to_z = z_copies(lambda t: t_send.at[t], lambda d: d1.at[z], dz_s, dz_r)
    start(to_z)
    d1[z] = t_send[z]
    arrived(to_z)
    to_xy = xy_copies(lambda t: d1.at[:, t], lambda d: d2.at[xy], dx_s, dx_r)
    start(to_xy)
    d2[xy] = d1[:, xy]
    arrived(to_xy)
    sent(to_z)
    sent(to_xy)

    def collect(i, carry):
        t2d[pl.ds(i, 1), :] = d2[i // NZ, lax.rem(i, NZ)]
        return carry

    lax.fori_loop(0, 128, collect, 0)
    got = jnp.transpose(t2d[...])
    chosen = got[0:64] * 32.0 + got[64:128] - 1.0

    def group_rows(c, g, t):
        return hid.at[c, pl.ds(pl.multiple_of(g * U + t * R, R), R), :]

    def rs_xy(c, g):
        return xy_copies(
            lambda t: p_sc.at[c, pl.ds(pl.multiple_of(g * U + t * R, R), R), :],
            lambda d: r1.at[c, g, d], cx_s.at[2 * c, g], cx_r.at[2 * c, g],
        )

    def rs_z(c, g):
        return z_copies(
            lambda t: q_sc.at[c, g, t], lambda d: r2.at[c, g, d], cz_s.at[2 * c, g], cz_r.at[2 * c, g]
        )

    def own_piece(c, g):
        rows = pl.ds(pl.multiple_of(g * U + xy * R, R), R)
        return hid.at[c, rows, pl.ds(pl.multiple_of(z * 128, 128), 128)]

    def ag_z(c, g):
        return z_copies(
            lambda t: own_piece(c, g), lambda d: own_piece(c, g), cz_s.at[2 * c + 1, g], cz_r.at[2 * c + 1, g]
        )

    def ag_xy(c, g):
        return xy_copies(
            lambda t: group_rows(c, g, xy), lambda d: group_rows(c, g, xy),
            cx_s.at[2 * c + 1, g], cx_r.at[2 * c + 1, g],
        )

    def partial_inputs(c, g, visible):
        p_sc[c, g * U : (g + 1) * U] = dot(visible, w_sc[...], 0, 0).astype(BF16)
        start(rs_xy(c, g))

    def plane_sum(c, g):
        arrived(rs_xy(c, g))
        rows = pl.ds(pl.multiple_of(g * U + xy * R, R), R)
        for f in range(NZ):
            cut = slice(f * 128, (f + 1) * 128)
            total = p_sc[c, rows, cut].astype(F32)
            for d in range(1, NXY):
                total = total + r1[c, g, d, :, cut].astype(F32)
            q_sc[c, g, f] = total.astype(BF16)
        start(rs_z(c, g))

    def ring_sum(c, g):
        arrived(rs_z(c, g))
        total = q_sc[c, g, z].astype(F32)
        for d in range(1, NZ):
            total = total + r2[c, g, d].astype(F32)
        value = 1.0 / (1.0 + jnp.exp(-(total + hb_ref[z])))
        own_piece(c, g)[...] = value.astype(BF16)
        start(ag_z(c, g))
        return value

    def ring_gather(c, g):
        arrived(ag_z(c, g))
        start(ag_xy(c, g))

    def users_of(g):
        return slice(g * U, (g + 1) * U)

    for g in range(GROUPS):
        for u in range(g * U // 128, (g + 1) * U // 128):
            picks = [chosen[u * 16 + k : u * 16 + k + 1] for k in range(CAP)]

            def block(b, carry, picks=picks, u=u):
                base = pl.multiple_of(b * 48, 48)
                at = (lax.broadcasted_iota(jnp.int32, (48, 128), 0) + base).astype(F32)
                hit = picks[0] == at
                for p in picks[1:]:
                    hit = hit | (p == at)
                s_sc[pl.ds(base, 48), u * 128 : (u + 1) * 128] = jnp.where(hit, 1.0, 0.0).astype(BF16)
                return carry

            lax.fori_loop(0, COLS // 48, block, 0)
        partial_inputs(0, g, s_sc[:, users_of(g)])
    for g in range(GROUPS):
        plane_sum(0, g)
    for g in range(GROUPS):
        pos_own[g] = ring_sum(0, g)
    for g in range(GROUPS):
        ring_gather(0, g)
    for g in range(GROUPS):
        arrived(ag_xy(0, g))
        l_sc[...] = dot(w_sc[...], hid[0, users_of(g)], 1, 1)

        def softmax(b, carry, g=g):
            base = pl.multiple_of(b * 16, 16)
            for h in range(U // 128):
                lanes = slice(h * 128, (h + 1) * 128)
                out_lanes = slice(g * U + h * 128, g * U + (h + 1) * 128)
                at = [pl.ds(pl.multiple_of(k * PAD + base, 16), 16) for k in range(LEVELS)]
                logits = [l_sc[a, lanes] + vbc[a, :] for a in at]
                largest = functools.reduce(jnp.maximum, logits)
                powers = [jnp.exp(v - largest) for v in logits]
                whole = functools.reduce(jnp.add, powers)
                rated = functools.reduce(jnp.add, [s_sc[a, out_lanes].astype(F32) for a in at])
                for a, v in zip(at, powers):
                    soft = (v / whole).astype(BF16)
                    r_sc[a, out_lanes] = (soft.astype(F32) * rated).astype(BF16)
            return carry

        lax.fori_loop(0, PAD // 16, softmax, 0)
        partial_inputs(1, g, r_sc[:, users_of(g)])

    ones = jnp.ones((8, USERS), BF16)
    vg_own = dot(ones, s_sc[...], 1, 1) - dot(ones, r_sc[...], 1, 1)
    vco[0] = vg_own
    vg_copy = pltpu.make_async_remote_copy(
        vco.at[0], vco.at[1], co_s.at[LEVELS], co_r.at[LEVELS], device_id=other, device_id_type=MESH
    )
    vg_copy.start()
    for k in range(LEVELS):
        acc_sc[k] = dot(s_sc[k * PAD : (k + 1) * PAD], hid[0], 1, 0)
    for u in range(4):
        at = pl.multiple_of(u * 128 + xy // 2 * 16, 16)
        block_rows = hid[0, pl.ds(at, 16), :].astype(F32)
        mine = lax.broadcasted_iota(jnp.int32, (16, F), 0) == lax.rem(xy, 2) * 8 + z
        ph_ref[u : u + 1] = jnp.sum(jnp.where(mine, block_rows, 0.0), axis=0, keepdims=True)

    for g in range(GROUPS):
        plane_sum(1, g)
    change = jnp.zeros((1, 128), F32)
    for g in range(GROUPS):
        value = ring_sum(1, g)
        change = change + jnp.sum(pos_own[g] - value, axis=0, keepdims=True)
    hz[z] = change
    h_z = z_copies(lambda t: hz.at[z], lambda d: hz.at[z], hz_s, hz_r)
    start(h_z)
    for g in range(GROUPS):
        ring_gather(1, g)
    arrived(h_z)
    hxy[xy] = hz[...]
    h_xy = xy_copies(lambda t: hxy.at[xy], lambda d: hxy.at[xy], hx_s, hx_r)
    start(h_xy)
    arrived(h_xy)
    total = hxy[0]
    for d in range(1, NXY):
        total = total + hxy[d]
    hco[0] = total
    hg_copy = pltpu.make_async_remote_copy(
        hco.at[0], hco.at[1], co_s.at[LEVELS + 1], co_r.at[LEVELS + 1], device_id=other, device_id_type=MESH
    )
    hg_copy.start()
    for g in range(GROUPS):
        arrived(ag_xy(1, g))

    wg_copies = []
    for k in range(LEVELS):
        grad = acc_sc[k] - dot(r_sc[k * PAD : (k + 1) * PAD], hid[1], 1, 0)
        own_sc[k] = grad.astype(BF16)
        copy = pltpu.make_async_remote_copy(
            own_sc.at[k], oth_sc.at[k], co_s.at[k], co_r.at[k], device_id=other, device_id_type=MESH
        )
        copy.start()
        wg_copies.append(copy)
    hg_copy.wait_recv()
    hg_ref[...] = hco[0] + hco[1]
    vg_copy.wait_recv()
    vg_ref[...] = vco[0] + vco[1]
    for k in range(LEVELS):
        wg_copies[k].wait_recv()
        wg_ref[k] = own_sc[k, 0:MOV].astype(F32) + oth_sc[k, 0:MOV].astype(F32)
    for c in range(2):
        for g in range(GROUPS):
            for copies in (rs_xy(c, g), rs_z(c, g), ag_z(c, g), ag_xy(c, g)):
                sent(copies)
    sent(h_z)
    sent(h_xy)
    for copy in (*wg_copies, hg_copy, vg_copy):
        copy.wait_send()


def on_device(movie_ids, ratings, valid, weights, vis_bias, hid_bias):
    dma = pltpu.SemaphoreType.DMA
    wg, vg, hg, ph = pl.pallas_call(
        kernel,
        out_shape=(
            jax.ShapeDtypeStruct((LEVELS, MOV, F), F32),
            jax.ShapeDtypeStruct((8, COLS), F32),
            jax.ShapeDtypeStruct((NZ, 1, 128), F32),
            jax.ShapeDtypeStruct((4, F), F32),
        ),
        in_specs=[pl.BlockSpec(memory_space=pltpu.VMEM)] * 6,
        out_specs=(pl.BlockSpec(memory_space=pltpu.VMEM),) * 4,
        scratch_shapes=[
            pltpu.VMEM((COLS, F), BF16),
            pltpu.VMEM((8, 256), F32),
            pltpu.VMEM((COLS, 128), F32),
            pltpu.VMEM((128, 128), F32),
            pltpu.VMEM((NZ, NXY, 1, 128), F32),
            pltpu.VMEM((NZ, NXY, 1, 128), F32),
            pltpu.VMEM((NXY, NZ, 1, 128), F32),
            pltpu.VMEM((COLS, USERS), BF16),
            pltpu.VMEM((COLS, USERS), BF16),
            pltpu.VMEM((COLS, U), F32),
            pltpu.VMEM((2, USERS, F), BF16),
            pltpu.VMEM((2, GROUPS, NXY, R, F), BF16),
            pltpu.VMEM((2, GROUPS, NZ, R, 128), BF16),
            pltpu.VMEM((2, GROUPS, NZ, R, 128), BF16),
            pltpu.VMEM((2, USERS, F), BF16),
            pltpu.VMEM((GROUPS, R, 128), F32),
            pltpu.VMEM((LEVELS, PAD, F), F32),
            pltpu.VMEM((LEVELS, PAD, F), BF16),
            pltpu.VMEM((LEVELS, PAD, F), BF16),
            pltpu.VMEM((NZ, 1, 128), F32),
            pltpu.VMEM((NXY, NZ, 1, 128), F32),
            pltpu.VMEM((2, NZ, 1, 128), F32),
            pltpu.VMEM((2, 8, COLS), F32),
            dma((NZ,)), dma((NZ,)), dma((NXY,)), dma((NXY,)),
            dma((4, GROUPS, NZ)), dma((4, GROUPS, NZ)), dma((4, GROUPS, NXY)), dma((4, GROUPS, NXY)),
            dma((NZ,)), dma((NZ,)), dma((NXY,)), dma((NXY,)),
            dma((LEVELS + 2,)), dma((LEVELS + 2,)),
        ],
        compiler_params=pltpu.CompilerParams(
            collective_id=0, has_side_effects=True, vmem_limit_bytes=50 << 20
        ),
    )(movie_ids, ratings, valid, weights, vis_bias, hid_bias.reshape(NZ, 1, 128))
    visible_grad = vg[0].reshape(LEVELS, PAD)[:, :MOV]
    return wg, visible_grad, hg.reshape(F), ph


def solution(mesh):
    split = Mesh(mesh.devices.reshape(NZ, 4, 4, mesh.shape["user"]), ALL)
    owner = ("z", "y", "x")
    in_specs = (P(ALL, None), P(ALL, None), P(ALL, None), P(None, owner, None), P(None, owner), P())
    out_specs = (P(None, owner, None), P(None, owner), P(), P(ALL, None))
    return jax.shard_map(on_device, mesh=split, in_specs=in_specs, out_specs=out_specs, check_vma=False)
```

time: 273 us -> 106 us (0.39)
  Pallas kernels: 0 us -> 95 us
  blocking collectives: 78.1 us -> 0 us
  local copies, waits for them, and re-layouts: 80.1 us -> 10.5 us
  starting transfers between devices: 47.7 us -> 0 us
  waiting for transfers between devices: 38.5 us -> 0 us
  other arithmetic: 13.5 us -> 0 us
  matrix products: 12.9 us -> 0 us
    pallas_call x0 -> x1, Pallas kernels: none -> 95 us  [on_device(): pl.pallas_call(kernel, out_shape=(jax.ShapeDtypeStruct((LEVELS, MOV, F),...]
    all_to_all x6 -> x0, blocking collectives: 78.1 us -> none  [the longest x4 50.5 us: from_everyone(): lax.all_to_all(jnp.broadcast_to(x[None], (devices, *x.shape)), axis, 0, 0...]
    scatter x2 -> x0, local copies, waits for them, and re-layouts: 49.2 us -> none  [the longest x1 24.6 us: on_device(): jnp.full((owners, capacity), -1, jnp.int32).at[target, placed]]
    all_to_all x7 -> x0, starting transfers between devices: 47.7 us -> none  [the longest x4 23.5 us: from_everyone(): lax.all_to_all(jnp.broadcast_to(x[None], (devices, *x.shape)), axis, 0, 0...]
    all_to_all x7 -> x0, waiting for transfers between devices: 38.5 us -> none  [the longest x4 15.3 us: from_everyone(): lax.all_to_all(jnp.broadcast_to(x[None], (devices, *x.shape)), axis, 0, 0...]
    dot_general x6 -> x0, matrix products: 12.9 us -> none  [the longest x2 4.12 us: hidden_phase(): jnp.dot(visible, weight_table, preferred_element_type=jnp.float32)]
    reduce_sum x13 -> x0, other arithmetic: 9.39 us -> none  [the longest x1 3.1 us: on_device(): jnp.sum(reconstructed_ratings.astype(jnp.float32), axis=0)]
    another operation x8 -> x1, local copies, waits for them, and re-layouts: 7.3 us -> 0.67 us  [on_device(): visible_grad = vg[0].reshape(LEVELS, PAD)[:, :MOV]]
  transfers between devices with their start and end apart: 7 -> 0, of which waited for: 7 -> 0; matrix products, arithmetic and copies ran while one was open for 7% -> 0% of each run, Pallas kernels for 0% -> 0%
where the time goes in v1:
time: 106 us
  Pallas kernels  95 us (90%)
  local copies, waits for them, and re-layouts  10.5 us (10%)
    pallas_call x1, Pallas kernels, on_device(): pl.pallas_call(kernel, out_shape=(jax.ShapeDtypeStruct((LEVELS, MOV, F),...  95 us
    unnamed x15, local copies, waits for them, and re-layouts  9.81 us

profile of v1, /device:TPU:1, one launch (start us, length us, event | category | flops | bytes accessed | tf_op | source)
XLA Modules:
  0.0 106.2 jit_solution(2310068895297664003)
XLA Ops:
  0.6 0.0 copy-start
  0.6 1.4 %copy-done = bf16[5,140,1024]{2,1,0:T(8,128)(2,1)S(1)} copy-done((bf16[5,140,1024]{2,1,0:T(8,128)(2,1)S(1)}, bf16[5,140,1024]{2,1,0:T(8,128)(2,1)}, u32[]{:S(2)}) %copy-start) | copy-done | bytes 1433624
  2.0 0.0 copy-start.1
  2.0 0.7 copy-done.1
  2.7 0.0 copy-start.2
  2.7 0.7 copy-done.2
  3.4 0.0 copy-start.3
  3.4 0.7 copy-done.3
  4.1 0.0 copy-start.4
  4.1 0.7 copy-done.4
  4.8 0.0 copy-start.5
  4.8 0.7 copy-done.5
  5.4 95.0 %shard_map.93 = (f32[5,140,1024]{2,1,0:T(8,128)}, f32[8,720]{1,0:T(8,128)S(1)}, f32[8,1,128]{2,1,0:T(1,128)S(1)}, f32[4,1024]{1,0:T(4,128)S(1)}) custom-call(s32[4,128]{1,0:T(4,128)S(1)} %copy-done.3, s32[4,128]{1,0:T(4,128)S(1)} %copy-done.4, s32[4,128]{1,0:T(4,128)S(1)} %copy-done.5, bf16[5,140,1024]{2,1,0:T(8,128)(2,1)S(1)} %copy-done, ...), custom_call_target="tpu_custom_call" | custom-call | tf_op jit(solution)/shard_map/pallas_call | solution.py:334
  100.5 0.7 reshape_squeeze.3
  101.2 3.8 %copy.13 = f32[5,140,1024]{2,1,0:T(8,128)} copy(f32[5,140,1024]{2,1,0:T(8,128)} %get-tuple-element.16) | data formatting | bytes 5734400
  105.0 0.6 copy.14
  105.6 0.6 copy.15
  (1 shorter events, 0.0 us)
Async XLA Ops:
  0.6 1.4 %copy-start = (bf16[5,140,1024]{2,1,0:T(8,128)(2,1)S(1)}, bf16[5,140,1024]{2,1,0:T(8,128)(2,1)}, u32[]{:S(2)}) copy-start(bf16[5,140,1024]{2,1,0:T(8,128)(2,1)} %w_ref.1) | copy-start | bytes 4300804
  2.0 0.7 copy-start.1
  2.7 0.7 copy-start.2
  3.4 0.7 copy-start.3
  4.1 0.7 copy-start.4
  4.8 0.7 copy-start.5

commit v2 on v1

--- a/solution.py
+++ b/solution.py
@@ -29,11 +29,11 @@
 
 
 def kernel(
-    ids_ref, rat_ref, val_ref, w_ref, vb_ref, hb_ref,
-    wg_ref, vg_ref, hg_ref, ph_ref,
+    ids_hbm, rat_hbm, val_hbm, w_hbm, vb_hbm, hb_hbm,
+    own_sc, oth_sc, vco, hco, ph_ref,
+    ids_ref, rat_ref, val_ref, w_ref, vb_ref, hb_ref, in_sem,
     w_sc, vb_pad, vbc, t2d, t_send, d1, d2, s_sc, r_sc, l_sc,
-    p_sc, r1, q_sc, r2, hid, pos_own, acc_sc, own_sc, oth_sc,
-    hz, hxy, hco, vco,
+    p_sc, r1, q_sc, r2, hid, pos_own, acc_sc, hz, hxy,
     dz_s, dz_r, dx_s, dx_r, cz_s, cz_r, cx_s, cx_r, hz_s, hz_r, hx_s, hx_r, co_s, co_r,
 ):
     z, y, x, core = [lax.axis_index(a) for a in ALL]
@@ -75,7 +75,10 @@
 
         lax.fori_loop(1, n, step, 0)
 
+    started = []
+
     def start(copies):
+        started.append(copies)
         each(copies, lambda c: c.start())
 
     def arrived(copies):
@@ -83,6 +86,18 @@
 
     def sent(copies):
         each(copies, lambda c: c.wait_send())
+
+    inputs = [
+        pltpu.make_async_copy(src, dst, in_sem.at[i])
+        for i, (src, dst) in enumerate(
+            (
+                (ids_hbm, ids_ref), (rat_hbm, rat_ref), (val_hbm, val_ref),
+                (w_hbm, w_ref), (vb_hbm, vb_ref), (hb_hbm, hb_ref),
+            )
+        )
+    ]
+    for copy in inputs:
+        copy.start()
 
     barrier = pltpu.get_barrier_semaphore()
 
@@ -99,6 +114,8 @@
     lax.fori_loop(1, NXY, greet_xy, 0)
     pl.semaphore_signal(barrier, 1, device_id=other, device_id_type=MESH)
 
+    for copy in inputs[:3]:
+        copy.wait()
     ids = ids_ref[...]
     owner = jnp.floor((ids.astype(F32) + 0.5) * (1.0 / MOV)).astype(jnp.int32)
     column = rat_ref[...] * PAD + (ids - owner * MOV) + 1
@@ -126,6 +143,8 @@
 
     lax.fori_loop(0, 128, spread, 0)
 
+    for copy in inputs[3:]:
+        copy.wait()
     for k in range(LEVELS):
         w_sc[k * PAD + 128 : (k + 1) * PAD] = jnp.zeros((PAD - 128, F), BF16)
         w_sc[k * PAD : k * PAD + MOV] = w_ref[k]
@@ -145,8 +164,6 @@
     start(to_xy)
     d2[xy] = d1[:, xy]
     arrived(to_xy)
-    sent(to_z)
-    sent(to_xy)
 
     def collect(i, carry):
         t2d[pl.ds(i, 1), :] = d2[i // NZ, lax.rem(i, NZ)]
@@ -159,12 +176,14 @@
     def group_rows(c, g, t):
         return hid.at[c, pl.ds(pl.multiple_of(g * U + t * R, R), R), :]
 
+    @functools.cache
     def rs_xy(c, g):
         return xy_copies(
             lambda t: p_sc.at[c, pl.ds(pl.multiple_of(g * U + t * R, R), R), :],
             lambda d: r1.at[c, g, d], cx_s.at[2 * c, g], cx_r.at[2 * c, g],
         )
 
+    @functools.cache
     def rs_z(c, g):
         return z_copies(
             lambda t: q_sc.at[c, g, t], lambda d: r2.at[c, g, d], cz_s.at[2 * c, g], cz_r.at[2 * c, g]
@@ -174,11 +193,13 @@
         rows = pl.ds(pl.multiple_of(g * U + xy * R, R), R)
         return hid.at[c, rows, pl.ds(pl.multiple_of(z * 128, 128), 128)]
 
+    @functools.cache
     def ag_z(c, g):
         return z_copies(
             lambda t: own_piece(c, g), lambda d: own_piece(c, g), cz_s.at[2 * c + 1, g], cz_r.at[2 * c + 1, g]
         )
 
+    @functools.cache
     def ag_xy(c, g):
         return xy_copies(
             lambda t: group_rows(c, g, xy), lambda d: group_rows(c, g, xy),
@@ -262,8 +283,10 @@
         partial_inputs(1, g, r_sc[:, users_of(g)])
 
     ones = jnp.ones((8, USERS), BF16)
-    vg_own = dot(ones, s_sc[...], 1, 1) - dot(ones, r_sc[...], 1, 1)
-    vco[0] = vg_own
+    for k in range(LEVELS):
+        level = slice(k * PAD, (k + 1) * PAD)
+        moved = dot(ones, s_sc[level], 1, 1) - dot(ones, r_sc[level], 1, 1)
+        vco[0, k : k + 1] = moved[0:1]
     vg_copy = pltpu.make_async_remote_copy(
         vco.at[0], vco.at[1], co_s.at[LEVELS], co_r.at[LEVELS], device_id=other, device_id_type=MESH
     )
@@ -312,36 +335,51 @@
         )
         copy.start()
         wg_copies.append(copy)
-    hg_copy.wait_recv()
-    hg_ref[...] = hco[0] + hco[1]
-    vg_copy.wait_recv()
-    vg_ref[...] = vco[0] + vco[1]
-    for k in range(LEVELS):
-        wg_copies[k].wait_recv()
-        wg_ref[k] = own_sc[k, 0:MOV].astype(F32) + oth_sc[k, 0:MOV].astype(F32)
-    for c in range(2):
-        for g in range(GROUPS):
-            for copies in (rs_xy(c, g), rs_z(c, g), ag_z(c, g), ag_xy(c, g)):
-                sent(copies)
-    sent(h_z)
-    sent(h_xy)
+    for copy in (hg_copy, vg_copy, *wg_copies):
+        copy.wait_recv()
+    for copies in started:
+        sent(copies)
     for copy in (*wg_copies, hg_copy, vg_copy):
         copy.wait_send()
 
 
+def finish(own_ref, oth_ref, vco_ref, hco_ref, ph_ref, wg_out, vg_out, hg_out, ph_out, wg, vg, hg, sem):
+    copies = []
+    for i, (src, dst) in enumerate(((ph_ref, ph_out), (vg, vg_out), (hg, hg_out))):
+        copies.append(pltpu.make_async_copy(src, dst, sem.at[i]))
+    copies[0].start()
+    vg[...] = (vco_ref[0] + vco_ref[1])[0:LEVELS, 0:MOV]
+    copies[1].start()
+    hg[...] = hco_ref[0] + hco_ref[1]
+    copies[2].start()
+    for k in range(LEVELS):
+        wg[k] = own_ref[k, 0:MOV].astype(F32) + oth_ref[k, 0:MOV].astype(F32)
+        copies.append(pltpu.make_async_copy(wg.at[k], wg_out.at[k], sem.at[3 + k]))
+        copies[-1].start()
+    for copy in copies:
+        copy.wait()
+
+
 def on_device(movie_ids, ratings, valid, weights, vis_bias, hid_bias):
     dma = pltpu.SemaphoreType.DMA
-    wg, vg, hg, ph = pl.pallas_call(
+    vmem = pl.BlockSpec(memory_space=pltpu.VMEM)
+    hbm = pl.BlockSpec(memory_space=pltpu.HBM)
+    shape = jax.ShapeDtypeStruct
+    parts = pl.pallas_call(
         kernel,
         out_shape=(
-            jax.ShapeDtypeStruct((LEVELS, MOV, F), F32),
-            jax.ShapeDtypeStruct((8, COLS), F32),
-            jax.ShapeDtypeStruct((NZ, 1, 128), F32),
-            jax.ShapeDtypeStruct((4, F), F32),
+            shape((LEVELS, PAD, F), BF16),
+            shape((LEVELS, PAD, F), BF16),
+            shape((2, 8, PAD), F32),
+            shape((2, NZ, 1, 128), F32),
+            shape((4, F), F32),
         ),
-        in_specs=[pl.BlockSpec(memory_space=pltpu.VMEM)] * 6,
-        out_specs=(pl.BlockSpec(memory_space=pltpu.VMEM),) * 4,
+        in_specs=[hbm] * 6,
+        out_specs=(vmem,) * 5,
         scratch_shapes=[
+            pltpu.VMEM((4, 128), jnp.int32), pltpu.VMEM((4, 128), jnp.int32), pltpu.VMEM((4, 128), jnp.int32),
+            pltpu.VMEM((LEVELS, MOV, F), BF16), pltpu.VMEM((LEVELS, MOV), F32), pltpu.VMEM((NZ, 1, 128), F32),
+            dma((6,)),
             pltpu.VMEM((COLS, F), BF16),
             pltpu.VMEM((8, 256), F32),
             pltpu.VMEM((COLS, 128), F32),
@@ -359,23 +397,31 @@
             pltpu.VMEM((2, USERS, F), BF16),
             pltpu.VMEM((GROUPS, R, 128), F32),
             pltpu.VMEM((LEVELS, PAD, F), F32),
-            pltpu.VMEM((LEVELS, PAD, F), BF16),
-            pltpu.VMEM((LEVELS, PAD, F), BF16),
             pltpu.VMEM((NZ, 1, 128), F32),
             pltpu.VMEM((NXY, NZ, 1, 128), F32),
-            pltpu.VMEM((2, NZ, 1, 128), F32),
-            pltpu.VMEM((2, 8, COLS), F32),
             dma((NZ,)), dma((NZ,)), dma((NXY,)), dma((NXY,)),
             dma((4, GROUPS, NZ)), dma((4, GROUPS, NZ)), dma((4, GROUPS, NXY)), dma((4, GROUPS, NXY)),
             dma((NZ,)), dma((NZ,)), dma((NXY,)), dma((NXY,)),
             dma((LEVELS + 2,)), dma((LEVELS + 2,)),
         ],
         compiler_params=pltpu.CompilerParams(
-            collective_id=0, has_side_effects=True, vmem_limit_bytes=50 << 20
+            collective_id=0, has_side_effects=True, vmem_limit_bytes=36 << 20
         ),
-    )(movie_ids, ratings, valid, weights, vis_bias, hid_bias.reshape(NZ, 1, 128))
-    visible_grad = vg[0].reshape(LEVELS, PAD)[:, :MOV]
-    return wg, visible_grad, hg.reshape(F), ph
+    )(*[
+        pltpu.with_memory_space_constraint(a, pltpu.HBM)
+        for a in (movie_ids, ratings, valid, weights, vis_bias, hid_bias.reshape(NZ, 1, 128))
+    ])
+    wg, vg, hg, ph = pl.pallas_call(
+        finish,
+        out_shape=(shape((LEVELS, MOV, F), F32), shape((LEVELS, MOV), F32), shape((NZ, 1, 128), F32), shape((4, F), F32)),
+        in_specs=[vmem] * 5,
+        out_specs=(hbm,) * 4,
+        scratch_shapes=[
+            pltpu.VMEM((LEVELS, MOV, F), F32), pltpu.VMEM((LEVELS, MOV), F32), pltpu.VMEM((NZ, 1, 128), F32), dma((8,)),
+        ],
+        compiler_params=pltpu.CompilerParams(vmem_limit_bytes=8 << 20),
+    )(*parts)
+    return wg, vg, hg.reshape(F), ph
 
 
 def solution(mesh):

time: 106 us -> 96.5 us (0.910)
  local copies, waits for them, and re-layouts: 10.5 us -> 0 us
    unnamed x15 -> x0, local copies, waits for them, and re-layouts: 9.81 us -> none
    pallas_call x1 -> x2, Pallas kernels: 95 us -> 95.8 us  [the longest x1 94 us: on_device(): pl.pallas_call(kernel, out_shape=(shape((LEVELS, PAD, F), BF16), shape((L...]
where the time goes in v2:
time: 96.5 us; the launch traced here: 96.4 us
  Pallas kernels  95.8 us (99%)
    pallas_call x1, Pallas kernels, on_device(): pl.pallas_call(kernel, out_shape=(shape((LEVELS, PAD, F), BF16), shape((L...  94 us

profile of v2, /device:TPU:1, one launch (start us, length us, event | category | flops | bytes accessed | tf_op | source)
XLA Modules:
  0.0 96.4 jit_solution(14723139544481496463)
XLA Ops:
  0.6 94.0 %shard_map.93 = (bf16[5,144,1024]{2,1,0:T(8,128)(2,1)S(1)}, bf16[5,144,1024]{2,1,0:T(8,128)(2,1)S(1)}, f32[2,8,144]{2,1,0:T(8,128)S(1)}, f32[2,8,1,128]{3,2,1,0:T(1,128)S(1)}, f32[4,1024]{1,0:T(4,128)S(1)}) custom-call(s32[4,128]{1,0:T(4,128)} %ids_hbm.1, s32[4,128]{1,0:T(4,128)} %rat_hbm.1, s32[4,128]{1,0:T(4,128)} %val_hbm.1, bf16[5,140,1024]{2,1,0:T(8,128)(2,1)} %w_hbm.1, ...), custom_call_target="tpu_custom_call" | custom-call | tf_op jit(solution)/shard_map/pallas_call | solution.py:368
  94.7 1.7 %shard_map.94 = (f32[5,140,1024]{2,1,0:T(8,128)}, f32[5,140]{1,0:T(8,128)}, f32[8,1,128]{2,1,0:T(1,128)}, f32[4,1024]{1,0:T(4,128)}) custom-call(bf16[5,144,1024]{2,1,0:T(8,128)(2,1)S(1)} %get-tuple-element.13.own_ref, bf16[5,144,1024]{2,1,0:T(8,128)(2,1)S(1)} %get-tuple-element.14.oth_ref, f32[2,8,144]{2,1,0:T(8,128)S(1)} %get-tuple-element.15.vco_ref, ...), custom_call_target="tpu_custom_call" | custom-call | tf_op jit(solution)/shard_map/pallas_call | solution.py:414

commit v3 on v2

v3 whole, which is shorter than its diff:
```python
import functools

import jax
import jax.numpy as jnp
from jax import lax
from jax.experimental import pallas as pl
from jax.experimental.pallas import tpu as pltpu
from jax.sharding import Mesh
from jax.sharding import PartitionSpec as P

LEVELS = 5
MOV = 140
PAD = 144
COLS = LEVELS * PAD
F = 1024
NZ, NXY = 8, 16
CAP = 12
USERS = 512
BLOCKS = USERS // 8
GROUPS = ((0, 128, True), (128, 128, False), (256, 128, False), (384, 128, False))
SUM_ORDER = (0, 1, 2, 3)
BATCHES = ((0, 1), (2, 3))
MOST = max(n for _, n, _ in GROUPS)
WIDEST = 256
ALL = ("z", "y", "x", "core")
MESH = pl.DeviceIdType.MESH
F32, BF16 = jnp.float32, jnp.bfloat16


def dot(a, b, ca, cb):
    return lax.dot_general(a, b, (((ca,), (cb,)), ((), ())), preferred_element_type=F32)


def kernel(
    ids_hbm, rat_hbm, val_hbm, w_hbm, vb_hbm, hb_hbm,
    own_sc, oth_sc, vco, hco, ph_ref,
    ids_ref, rat_ref, val_ref, w_ref, vb_ref, hb_ref, in_sem,
    w_sc, vb_pad, vbc, t2d, t_send, d1, d2, s_sc, r_sc, l_sc,
    p_sc, r1, q_sc, r2, hid, flat, pos_own, acc_sc, hz, hxy,
    dz_s, dz_r, dx_s, dx_r, cz_s, cz_r, cx_s, cx_r, hz_s, hz_r, hx_s, hx_r, co_s, co_r,
):
    z, y, x, core = [lax.axis_index(a) for a in ALL]
    xy = y * 4 + x
    other = (z, y, x, 1 - core)

    def xy_peer(d):
        return lax.rem(y + d // 4, 4), lax.rem(x + lax.rem(d, 4), 4)

    def z_peer(d):
        return lax.rem(z + d, NZ)

    def xy_copies(src, dst, send, recv, whole):
        def copy(d):
            ty, tx = xy_peer(d)
            return pltpu.make_async_remote_copy(
                src(ty * 4 + tx), dst(d), send, recv, device_id=(z, ty, tx, core), device_id_type=MESH
            )

        return NXY, copy, send, recv, whole

    def z_copies(src, dst, send, recv, whole):
        def copy(d):
            tz = z_peer(d)
            return pltpu.make_async_remote_copy(
                src(tz), dst(d), send, recv, device_id=(tz, y, x, core), device_id_type=MESH
            )

        return NZ, copy, send, recv, whole

    started = []

    def start(copies):
        started.append(copies)
        n, copy = copies[:2]

        def step(d, carry):
            copy(d).start()
            return carry

        lax.fori_loop(1, n, step, 0)

    def all_of(copies):
        send, recv, whole = copies[2:]
        return pltpu.make_async_remote_copy(whole, whole, send, recv, device_id=other, device_id_type=MESH)

    def arrived(copies):
        all_of(copies).wait_recv()

    def sent(copies):
        all_of(copies).wait_send()

    inputs = [
        pltpu.make_async_copy(src, dst, in_sem.at[i])
        for i, (src, dst) in enumerate(
            (
                (ids_hbm, ids_ref), (rat_hbm, rat_ref), (val_hbm, val_ref),
                (w_hbm, w_ref), (vb_hbm, vb_ref), (hb_hbm, hb_ref),
            )
        )
    ]
    for copy in inputs:
        copy.start()

    barrier = pltpu.get_barrier_semaphore()

    def greet_xy(d, carry):
        ty, tx = xy_peer(d)
        pl.semaphore_signal(barrier, 1, device_id=(z, ty, tx, core), device_id_type=MESH)
        return carry

    def greet_z(d, carry):
        pl.semaphore_signal(barrier, 1, device_id=(z_peer(d), y, x, core), device_id_type=MESH)
        return carry

    lax.fori_loop(1, NZ, greet_z, 0)
    lax.fori_loop(1, NXY, greet_xy, 0)
    pl.semaphore_signal(barrier, 1, device_id=other, device_id_type=MESH)

    for copy in inputs[:3]:
        copy.wait()
    ids = ids_ref[...]
    owner = jnp.floor((ids.astype(F32) + 0.5) * (1.0 / MOV)).astype(jnp.int32)
    column = rat_ref[...] * PAD + (ids - owner * MOV) + 1
    high = lax.shift_right_logical(column, 5).astype(F32)
    low = (column & 31).astype(F32)
    owner = jnp.where(val_ref[...] == 1, owner, -1)
    row = lax.broadcasted_iota(jnp.int32, (128, 128), 0)
    lane = lax.broadcasted_iota(jnp.int32, (128, 128), 1)
    before = jnp.where(row < lane, 1.0, 0.0).astype(BF16)
    rank_row = (row & 15).astype(F32)
    user_row = lax.shift_right_logical(row, 4) & 3
    hot = [jnp.where(owner[u : u + 1] == row, 1.0, 0.0) for u in range(4)]
    counts = dot(jnp.concatenate(hot, axis=0).astype(BF16), before, 1, 0)
    picks = []
    for u in range(4):
        rank = jnp.sum(hot[u] * counts[u * 128 : (u + 1) * 128], axis=0, keepdims=True)
        part = jnp.where(row < 64, high[u : u + 1], low[u : u + 1])
        picks.append(jnp.where((user_row == u) & (rank_row == rank), part, 0.0))
    table = dot(
        jnp.concatenate(hot, axis=1).astype(BF16), jnp.concatenate(picks, axis=1).astype(BF16), 1, 1
    )
    for i in range(NZ):
        for k in range(NXY):
            t_send[i, k] = table[i * NXY + k : i * NXY + k + 1]

    pl.semaphore_wait(barrier, NZ - 1 + NXY - 1 + 1)

    to_z = z_copies(
        lambda t: t_send.at[t], lambda d: d1.at[z], dz_s.at[0], dz_r.at[0], t_send.at[0 : NZ - 1]
    )
    start(to_z)
    d1[z] = t_send[z]
    for copy in inputs[3:]:
        copy.wait()
    for k in range(LEVELS):
        w_sc[k * PAD + 128 : (k + 1) * PAD] = jnp.zeros((PAD - 128, F), BF16)
        w_sc[k * PAD : k * PAD + MOV] = w_ref[k]
    vb_pad[...] = jnp.zeros((8, 256), F32)
    vb_pad[0:LEVELS, 0:MOV] = vb_ref[...]
    bias_columns = jnp.transpose(vb_pad[...])
    for k in range(LEVELS):
        vbc[k * PAD : (k + 1) * PAD] = jnp.broadcast_to(bias_columns[0:PAD, k : k + 1], (PAD, 128))

    arrived(to_z)
    to_xy = xy_copies(
        lambda t: d1.at[:, t], lambda d: d2.at[xy], dx_s.at[0], dx_r.at[0], d2.at[0 : NXY - 1]
    )
    start(to_xy)
    d2[xy] = d1[:, xy]
    arrived(to_xy)

    for i in range(NXY):
        for k in range(NZ):
            t2d[i * NZ + k : i * NZ + k + 1] = d2[i, k]
    got = jnp.transpose(t2d[...])
    chosen = got[0:64] * 32.0 + got[64:128] - 1.0

    def layout(g):
        first, users, ring_first = GROUPS[g]
        return first // 8, users // 128, ring_first

    def piece(t, g, first_stage):
        base, n, ring_first = layout(g)
        return pl.ds(base + t * n * (2 if ring_first and first_stage else 1), n * (2 if ring_first and first_stage else 1))

    def own_blocks(g):
        return piece(z if layout(g)[2] else xy, g, True)

    def own_chunk(g):
        return lax.rem(xy, NZ) if layout(g)[2] else z

    def own_piece(c, g):
        base, n, ring_first = layout(g)
        blocks = pl.ds(base + (z * 2 + xy // NZ) * n, n) if ring_first else own_blocks(g)
        return hid.at[c, blocks, :, pl.ds(pl.multiple_of(own_chunk(g) * 128, 128), 128)]

    def stage(c, half, g, is_wide, src, dst):
        k, ring = 2 * c + half, layout(g)[2] == is_wide
        base, n, _ = layout(g)
        count = (NZ if ring else NXY) - 1
        rows = n * (2 if layout(g)[2] else 1)
        whole = p_sc.at[c, pl.ds(base, count * rows)] if is_wide else q_sc.at[c, g, 0:count, 0:n]
        if ring:
            return z_copies(src, dst, cz_s.at[k, g], cz_r.at[k, g], whole)
        return xy_copies(src, dst, cx_s.at[k, g], cx_r.at[k, g], whole)

    @functools.cache
    def rs_wide(c, g):
        return stage(c, 0, g, True, lambda t: p_sc.at[c, piece(t, g, True)], lambda d: r1.at[c, piece(d, g, True)])

    @functools.cache
    def rs_narrow(c, g):
        n = layout(g)[1]
        return stage(c, 0, g, False, lambda t: q_sc.at[c, g, t, 0:n], lambda d: r2.at[c, g, d, 0:n])

    @functools.cache
    def ag_narrow(c, g):
        return stage(c, 1, g, False, lambda t: own_piece(c, g), lambda d: own_piece(c, g))

    @functools.cache
    def ag_wide(c, g):
        return stage(c, 1, g, True, lambda t: hid.at[c, own_blocks(g)], lambda d: hid.at[c, own_blocks(g)])

    def users_of(g):
        first, users, _ = GROUPS[g]
        return slice(first, first + users)

    def blocks_of(g):
        first, users, _ = GROUPS[g]
        return slice(first // 8, (first + users) // 8)

    def batch_users(b):
        return slice(users_of(b[0]).start, users_of(b[-1]).stop)

    def partial_inputs(c, b, visible):
        sums = dot(visible, w_sc[...], 0, 0)
        first = batch_users(b).start // 8
        p_sc[c, first : first + sums.shape[0] // 8] = sums.reshape(sums.shape[0] // 8, 8, F).astype(BF16)
        for g in b:
            start(rs_wide(c, g))

    def first_sum(c, g):
        arrived(rs_wide(c, g))
        n, ring_first = layout(g)[1:]
        for h in range(2 if ring_first else 1):
            for f in range(NZ):
                cut = slice(f * 128, (f + 1) * 128)
                base = layout(g)[0]
                mine = base + (z * 2 * n if ring_first else xy * n) + h * n
                total = p_sc[c, pl.ds(mine, n), :, cut].astype(F32)
                for d in range(1, NZ if ring_first else NXY):
                    slot = base + d * n * (2 if ring_first else 1) + h * n
                    total = total + r1[c, slot : slot + n, :, cut].astype(F32)
                q_sc[c, g, h * NZ + f, 0:n] = total.astype(BF16)
        start(rs_narrow(c, g))

    def second_sum(c, g):
        arrived(rs_narrow(c, g))
        n, ring_first = layout(g)[1:]
        total = q_sc[c, g, xy if ring_first else z, 0:n].astype(F32)
        for d in range(1, NXY if ring_first else NZ):
            total = total + r2[c, g, d, 0:n].astype(F32)
        value = 1.0 / (1.0 + jnp.exp(-(total + hb_ref[own_chunk(g)])))
        own_piece(c, g)[...] = value.astype(BF16)
        start(ag_narrow(c, g))
        return value

    def gather(c, g):
        arrived(ag_narrow(c, g))
        start(ag_wide(c, g))

    def gathered(c, g):
        arrived(ag_wide(c, g))
        rows = hid[c, blocks_of(g)].astype(F32)
        flat[c, users_of(g)] = rows.reshape(rows.shape[0] * 8, F).astype(BF16)

    for b in BATCHES:
        for u in range(batch_users(b).start // 128, batch_users(b).stop // 128):
            picks = [chosen[u * 16 + k : u * 16 + k + 1] for k in range(CAP)]

            def block(b, carry, picks=picks, u=u):
                base = pl.multiple_of(b * 48, 48)
                at = (lax.broadcasted_iota(jnp.int32, (48, 128), 0) + base).astype(F32)
                hit = picks[0] == at
                for p in picks[1:]:
                    hit = hit | (p == at)
                s_sc[pl.ds(base, 48), u * 128 : (u + 1) * 128] = jnp.where(hit, 1.0, 0.0).astype(BF16)
                return carry

            lax.fori_loop(0, COLS // 48, block, 0)
        partial_inputs(0, b, s_sc[:, batch_users(b)])
    for g in SUM_ORDER:
        first_sum(0, g)
    for g in SUM_ORDER:
        pos_own[g, 0 : layout(g)[1]] = second_sum(0, g)
    for g in SUM_ORDER:
        gather(0, g)
    for b in BATCHES:
        for g in b:
            gathered(0, g)
        first = batch_users(b).start
        users = batch_users(b).stop - first
        l_sc[:, 0:users] = dot(w_sc[...], flat[0, batch_users(b)], 1, 1)

        def softmax(i, carry, first=first, users=users):
            base = pl.multiple_of(i * 16, 16)
            for h in range(users // 128):
                lanes = slice(h * 128, (h + 1) * 128)
                out_lanes = slice(first + h * 128, first + (h + 1) * 128)
                at = [pl.ds(pl.multiple_of(k * PAD + base, 16), 16) for k in range(LEVELS)]
                logits = [l_sc[a, lanes] + vbc[a, :] for a in at]
                largest = functools.reduce(jnp.maximum, logits)
                powers = [jnp.exp(v - largest) for v in logits]
                whole = functools.reduce(jnp.add, powers)
                rated = functools.reduce(jnp.add, [s_sc[a, out_lanes].astype(F32) for a in at])
                scale = rated / whole
                for a, v in zip(at, powers):
                    r_sc[a, out_lanes] = (v * scale).astype(BF16)
            return carry

        lax.fori_loop(0, PAD // 16, softmax, 0)
        partial_inputs(1, b, r_sc[:, batch_users(b)])

    ones = jnp.ones((8, USERS), BF16)
    for k in range(LEVELS):
        level = slice(k * PAD, (k + 1) * PAD)
        moved = dot(ones, s_sc[level], 1, 1) - dot(ones, r_sc[level], 1, 1)
        vco[0, k : k + 1] = moved[0:1]
    vg_copy = pltpu.make_async_remote_copy(
        vco.at[0], vco.at[1], co_s.at[LEVELS], co_r.at[LEVELS], device_id=other, device_id_type=MESH
    )
    vg_copy.start()
    for k in range(LEVELS):
        acc_sc[k] = dot(s_sc[k * PAD : (k + 1) * PAD], flat[0], 1, 0)
    for u in range(4):
        block_rows = hid[0, u * 16 + xy].astype(F32)
        mine = lax.broadcasted_iota(jnp.int32, (8, F), 0) == z
        ph_ref[u : u + 1] = jnp.sum(jnp.where(mine, block_rows, 0.0), axis=0, keepdims=True)

    for g in SUM_ORDER:
        first_sum(1, g)
    change = [jnp.zeros((1, 128), F32), jnp.zeros((1, 128), F32)]
    for g in SUM_ORDER:
        value = second_sum(1, g)
        kind = 1 if layout(g)[2] else 0
        moved = jnp.sum(pos_own[g, 0 : layout(g)[1]] - value, axis=0)
        change[kind] = change[kind] + jnp.sum(moved, axis=0, keepdims=True)
    hz[z] = jnp.concatenate(change, axis=0)
    h_z = z_copies(lambda t: hz.at[z], lambda d: hz.at[z], hz_s.at[0], hz_r.at[0], hz.at[0 : NZ - 1])
    start(h_z)
    for g in SUM_ORDER:
        gather(1, g)
    arrived(h_z)
    rest = functools.reduce(jnp.add, [hz[k, 1:2] for k in range(NZ)])
    for k in range(NZ):
        hxy[xy, k] = hz[k, 0:1] + jnp.where(lax.rem(xy, NZ) == k, rest, 0.0)
    h_xy = xy_copies(
        lambda t: hxy.at[xy], lambda d: hxy.at[xy], hx_s.at[0], hx_r.at[0], hxy.at[0 : NXY - 1]
    )
    start(h_xy)
    arrived(h_xy)
    total = hxy[0]
    for d in range(1, NXY):
        total = total + hxy[d]
    hco[0] = total
    hg_copy = pltpu.make_async_remote_copy(
        hco.at[0], hco.at[1], co_s.at[LEVELS + 1], co_r.at[LEVELS + 1], device_id=other, device_id_type=MESH
    )
    hg_copy.start()
    for g in SUM_ORDER:
        gathered(1, g)

    wg_copies = []
    for k in range(LEVELS):
        grad = acc_sc[k] - dot(r_sc[k * PAD : (k + 1) * PAD], flat[1], 1, 0)
        own_sc[k] = grad.astype(BF16)
        copy = pltpu.make_async_remote_copy(
            own_sc.at[k], oth_sc.at[k], co_s.at[k], co_r.at[k], device_id=other, device_id_type=MESH
        )
        copy.start()
        wg_copies.append(copy)
    for copy in (hg_copy, vg_copy, *wg_copies):
        copy.wait_recv()
    for copies in started:
        sent(copies)
    for copy in (*wg_copies, hg_copy, vg_copy):
        copy.wait_send()


def finish(own_ref, oth_ref, vco_ref, hco_ref, ph_ref, wg_out, vg_out, hg_out, ph_out, wg, vg, hg, sem):
    copies = []
    for i, (src, dst) in enumerate(((ph_ref, ph_out), (vg, vg_out), (hg, hg_out))):
        copies.append(pltpu.make_async_copy(src, dst, sem.at[i]))
    copies[0].start()
    vg[...] = (vco_ref[0] + vco_ref[1])[0:LEVELS, 0:MOV]
    copies[1].start()
    hg[...] = hco_ref[0] + hco_ref[1]
    copies[2].start()
    for k in range(LEVELS):
        wg[k] = own_ref[k, 0:MOV].astype(F32) + oth_ref[k, 0:MOV].astype(F32)
        copies.append(pltpu.make_async_copy(wg.at[k], wg_out.at[k], sem.at[3 + k]))
        copies[-1].start()
    for copy in copies:
        copy.wait()


def on_device(movie_ids, ratings, valid, weights, vis_bias, hid_bias):
    dma = pltpu.SemaphoreType.DMA
    vmem = pl.BlockSpec(memory_space=pltpu.VMEM)
    hbm = pl.BlockSpec(memory_space=pltpu.HBM)
    shape = jax.ShapeDtypeStruct
    parts = pl.pallas_call(
        kernel,
        out_shape=(
            shape((LEVELS, PAD, F), BF16),
            shape((LEVELS, PAD, F), BF16),
            shape((2, 8, PAD), F32),
            shape((2, NZ, 1, 128), F32),
            shape((4, F), F32),
        ),
        in_specs=[hbm] * 6,
        out_specs=(vmem,) * 5,
        scratch_shapes=[
            pltpu.VMEM((4, 128), jnp.int32), pltpu.VMEM((4, 128), jnp.int32), pltpu.VMEM((4, 128), jnp.int32),
            pltpu.VMEM((LEVELS, MOV, F), BF16), pltpu.VMEM((LEVELS, MOV), F32), pltpu.VMEM((NZ, 1, 128), F32),
            dma((6,)),
            pltpu.VMEM((COLS, F), BF16),
            pltpu.VMEM((8, 256), F32),
            pltpu.VMEM((COLS, 128), F32),
            pltpu.VMEM((128, 128), F32),
            pltpu.VMEM((NZ, NXY, 1, 128), F32),
            pltpu.VMEM((NZ, NXY, 1, 128), F32),
            pltpu.VMEM((NXY, NZ, 1, 128), F32),
            pltpu.VMEM((COLS, USERS), BF16),
            pltpu.VMEM((COLS, USERS), BF16),
            pltpu.VMEM((COLS, WIDEST), F32),
            pltpu.VMEM((2, BLOCKS, 8, F), BF16),
            pltpu.VMEM((2, BLOCKS, 8, F), BF16),
            pltpu.VMEM((2, len(GROUPS), NXY, MOST // 128, 8, 128), BF16),
            pltpu.VMEM((2, len(GROUPS), NXY, MOST // 128, 8, 128), BF16),
            pltpu.VMEM((2, BLOCKS, 8, F), BF16),
            pltpu.VMEM((2, USERS, F), BF16),
            pltpu.VMEM((len(GROUPS), MOST // 128, 8, 128), F32),
            pltpu.VMEM((LEVELS, PAD, F), F32),
            pltpu.VMEM((NZ, 2, 128), F32),
            pltpu.VMEM((NXY, NZ, 1, 128), F32),
            *[dma((1,))] * 4, *[dma((4, len(GROUPS)))] * 4, *[dma((1,))] * 4,
            dma((LEVELS + 2,)), dma((LEVELS + 2,)),
        ],
        compiler_params=pltpu.CompilerParams(
            collective_id=0, has_side_effects=True, vmem_limit_bytes=36 << 20
        ),
    )(*[
        pltpu.with_memory_space_constraint(a, pltpu.HBM)
        for a in (movie_ids, ratings, valid, weights, vis_bias, hid_bias.reshape(NZ, 1, 128))
    ])
    wg, vg, hg, ph = pl.pallas_call(
        finish,
        out_shape=(shape((LEVELS, MOV, F), F32), shape((LEVELS, MOV), F32), shape((NZ, 1, 128), F32), shape((4, F), F32)),
        in_specs=[vmem] * 5,
        out_specs=(hbm,) * 4,
        scratch_shapes=[
            pltpu.VMEM((LEVELS, MOV, F), F32), pltpu.VMEM((LEVELS, MOV), F32), pltpu.VMEM((NZ, 1, 128), F32), dma((8,)),
        ],
        compiler_params=pltpu.CompilerParams(vmem_limit_bytes=8 << 20),
    )(*parts)
    return wg, vg, hg.reshape(F), ph


def solution(mesh):
    split = Mesh(mesh.devices.reshape(NZ, 4, 4, mesh.shape["user"]), ALL)
    owner = ("z", "y", "x")
    in_specs = (P(ALL, None), P(ALL, None), P(ALL, None), P(None, owner, None), P(None, owner), P())
    out_specs = (P(None, owner, None), P(None, owner), P(), P(ALL, None))
    return jax.shard_map(on_device, mesh=split, in_specs=in_specs, out_specs=out_specs, check_vma=False)
```

time: 96.5 us -> 83 us (0.86)
  Pallas kernels: 95.8 us -> 82.3 us
    pallas_call x1, Pallas kernels: 94 us -> 80.5 us  [on_device(): pl.pallas_call(kernel, out_shape=(shape((LEVELS, PAD, F), BF16), shape((L...]
where the time goes in v3:
time: 83 us; the launch traced here: 82.9 us
  Pallas kernels  82.3 us (99%)
    pallas_call x1, Pallas kernels, on_device(): pl.pallas_call(kernel, out_shape=(shape((LEVELS, PAD, F), BF16), shape((L...  80.5 us
    pallas_call x1, Pallas kernels, on_device(): pl.pallas_call(finish, out_shape=(shape((LEVELS, MOV, F), F32), shape((LE...  1.73 us

profile of v3, /device:TPU:1, one launch (start us, length us, event | category | flops | bytes accessed | tf_op | source)
XLA Modules:
  0.0 82.9 jit_solution(6198989232776261496)
XLA Ops:
  0.6 80.5 %shard_map.93 = (bf16[5,144,1024]{2,1,0:T(8,128)(2,1)S(1)}, bf16[5,144,1024]{2,1,0:T(8,128)(2,1)S(1)}, f32[2,8,144]{2,1,0:T(8,128)S(1)}, f32[2,8,1,128]{3,2,1,0:T(1,128)S(1)}, f32[4,1024]{1,0:T(4,128)S(1)}) custom-call(s32[4,128]{1,0:T(4,128)} %ids_hbm.1, s32[4,128]{1,0:T(4,128)} %rat_hbm.1, s32[4,128]{1,0:T(4,128)} %val_hbm.1, bf16[5,140,1024]{2,1,0:T(8,128)(2,1)} %w_hbm.1, ...), custom_call_target="tpu_custom_call" | custom-call | tf_op jit(solution)/shard_map/pallas_call | solution.py:412
  81.2 1.7 %shard_map.94 = (f32[5,140,1024]{2,1,0:T(8,128)}, f32[5,140]{1,0:T(8,128)}, f32[8,1,128]{2,1,0:T(1,128)}, f32[4,1024]{1,0:T(4,128)}) custom-call(bf16[5,144,1024]{2,1,0:T(8,128)(2,1)S(1)} %get-tuple-element.13.own_ref, bf16[5,144,1024]{2,1,0:T(8,128)(2,1)S(1)} %get-tuple-element.14.oth_ref, f32[2,8,144]{2,1,0:T(8,128)S(1)} %get-tuple-element.15.vco_ref, ...), custom_call_target="tpu_custom_call" | custom-call | tf_op jit(solution)/shard_map/pallas_call | solution.py:457

commit v4 on v3

--- a/solution.py
+++ b/solution.py
@@ -19,6 +19,7 @@
 BLOCKS = USERS // 8
 GROUPS = ((0, 128, True), (128, 128, False), (256, 128, False), (384, 128, False))
 SUM_ORDER = (0, 1, 2, 3)
+PIPE = ((0, 1), (0, 0), (0, 2), (1, 1), (0, 3), (1, 0), (1, 2), (2, 1), (1, 3), (2, 0), (2, 2), (2, 3))
 BATCHES = ((0, 1), (2, 3))
 MOST = max(n for _, n, _ in GROUPS)
 WIDEST = 256
@@ -33,11 +34,11 @@
 
 def kernel(
     ids_hbm, rat_hbm, val_hbm, w_hbm, vb_hbm, hb_hbm,
-    own_sc, oth_sc, vco, hco, ph_ref,
+    wg_ref, vg_ref, hco, ph_ref,
     ids_ref, rat_ref, val_ref, w_ref, vb_ref, hb_ref, in_sem,
     w_sc, vb_pad, vbc, t2d, t_send, d1, d2, s_sc, r_sc, l_sc,
     p_sc, r1, q_sc, r2, hid, flat, pos_own, acc_sc, hz, hxy,
-    dz_s, dz_r, dx_s, dx_r, cz_s, cz_r, cx_s, cx_r, hz_s, hz_r, hx_s, hx_r, co_s, co_r,
+    dz_s, dz_r, dx_s, dx_r, cz_s, cz_r, cx_s, cx_r, hz_s, hz_r, hx_s, hx_r, hc_s, hc_r, co_s, co_r,
 ):
     z, y, x, core = [lax.axis_index(a) for a in ALL]
     xy = y * 4 + x
@@ -221,6 +222,27 @@
     def ag_wide(c, g):
         return stage(c, 1, g, True, lambda t: hid.at[c, own_blocks(g)], lambda d: hid.at[c, own_blocks(g)])
 
+    shared = []
+
+    def share(mine, theirs):
+        i = len(shared)
+        copy = pltpu.make_async_remote_copy(
+            mine, mine, co_s.at[i], co_r.at[i], device_id=other, device_id_type=MESH
+        )
+        copy.start()
+        shared.append(
+            pltpu.make_async_remote_copy(
+                theirs, theirs, co_s.at[i], co_r.at[i], device_id=other, device_id_type=MESH
+            )
+        )
+
+    seen = []
+
+    def have_shared(upto):
+        for copy in shared[len(seen) : upto]:
+            copy.wait_recv()
+            seen.append(copy)
+
     def users_of(g):
         first, users, _ = GROUPS[g]
         return slice(first, first + users)
@@ -272,7 +294,8 @@
     def gathered(c, g):
         arrived(ag_wide(c, g))
         rows = hid[c, blocks_of(g)].astype(F32)
-        flat[c, users_of(g)] = rows.reshape(rows.shape[0] * 8, F).astype(BF16)
+        flat[c, core, users_of(g)] = rows.reshape(rows.shape[0] * 8, F).astype(BF16)
+        share(flat.at[c, core, users_of(g)], flat.at[c, 1 - core, users_of(g)])
 
     for b in BATCHES:
         for u in range(batch_users(b).start // 128, batch_users(b).stop // 128):
@@ -284,23 +307,25 @@
                 hit = picks[0] == at
                 for p in picks[1:]:
                     hit = hit | (p == at)
-                s_sc[pl.ds(base, 48), u * 128 : (u + 1) * 128] = jnp.where(hit, 1.0, 0.0).astype(BF16)
+                s_sc[core, pl.ds(base, 48), u * 128 : (u + 1) * 128] = jnp.where(hit, 1.0, 0.0).astype(BF16)
                 return carry
 
             lax.fori_loop(0, COLS // 48, block, 0)
-        partial_inputs(0, b, s_sc[:, batch_users(b)])
-    for g in SUM_ORDER:
-        first_sum(0, g)
-    for g in SUM_ORDER:
-        pos_own[g, 0 : layout(g)[1]] = second_sum(0, g)
-    for g in SUM_ORDER:
-        gather(0, g)
+        partial_inputs(0, b, s_sc[core, :, batch_users(b)])
+        share(s_sc.at[core, :, batch_users(b)], s_sc.at[1 - core, :, batch_users(b)])
+    for step, g in PIPE:
+        if step == 0:
+            first_sum(0, g)
+        elif step == 1:
+            pos_own[g, 0 : layout(g)[1]] = second_sum(0, g)
+        else:
+            gather(0, g)
     for b in BATCHES:
         for g in b:
             gathered(0, g)
         first = batch_users(b).start
         users = batch_users(b).stop - first
-        l_sc[:, 0:users] = dot(w_sc[...], flat[0, batch_users(b)], 1, 1)
+        l_sc[:, 0:users] = dot(w_sc[...], flat[0, core, batch_users(b)], 1, 1)
 
         def softmax(i, carry, first=first, users=users):
             base = pl.multiple_of(i * 16, 16)
@@ -312,33 +337,25 @@
                 largest = functools.reduce(jnp.maximum, logits)
                 powers = [jnp.exp(v - largest) for v in logits]
                 whole = functools.reduce(jnp.add, powers)
-                rated = functools.reduce(jnp.add, [s_sc[a, out_lanes].astype(F32) for a in at])
+                rated = functools.reduce(jnp.add, [s_sc[core, a, out_lanes].astype(F32) for a in at])
                 scale = rated / whole
                 for a, v in zip(at, powers):
-                    r_sc[a, out_lanes] = (v * scale).astype(BF16)
+                    r_sc[core, a, out_lanes] = (v * scale).astype(BF16)
             return carry
 
         lax.fori_loop(0, PAD // 16, softmax, 0)
-        partial_inputs(1, b, r_sc[:, batch_users(b)])
-
-    ones = jnp.ones((8, USERS), BF16)
-    for k in range(LEVELS):
-        level = slice(k * PAD, (k + 1) * PAD)
-        moved = dot(ones, s_sc[level], 1, 1) - dot(ones, r_sc[level], 1, 1)
-        vco[0, k : k + 1] = moved[0:1]
-    vg_copy = pltpu.make_async_remote_copy(
-        vco.at[0], vco.at[1], co_s.at[LEVELS], co_r.at[LEVELS], device_id=other, device_id_type=MESH
-    )
-    vg_copy.start()
-    for k in range(LEVELS):
-        acc_sc[k] = dot(s_sc[k * PAD : (k + 1) * PAD], flat[0], 1, 0)
-    for u in range(4):
-        block_rows = hid[0, u * 16 + xy].astype(F32)
-        mine = lax.broadcasted_iota(jnp.int32, (8, F), 0) == z
-        ph_ref[u : u + 1] = jnp.sum(jnp.where(mine, block_rows, 0.0), axis=0, keepdims=True)
+        partial_inputs(1, b, r_sc[core, :, batch_users(b)])
+        share(r_sc.at[core, :, batch_users(b)], r_sc.at[1 - core, :, batch_users(b)])
+
+    def columns(n):
+        return slice(n * 256, (n + 1) * 256)
 
     for g in SUM_ORDER:
         first_sum(1, g)
+
+    have_shared(len(shared))
+    for n in range(F // 256):
+        acc_sc[:, columns(n)] = dot(s_sc[0], flat[0, 0, :, columns(n)], 1, 0)
     change = [jnp.zeros((1, 128), F32), jnp.zeros((1, 128), F32)]
     for g in SUM_ORDER:
         value = second_sum(1, g)
@@ -348,8 +365,20 @@
     hz[z] = jnp.concatenate(change, axis=0)
     h_z = z_copies(lambda t: hz.at[z], lambda d: hz.at[z], hz_s.at[0], hz_r.at[0], hz.at[0 : NZ - 1])
     start(h_z)
+    for n in range(F // 256):
+        acc_sc[:, columns(n)] = acc_sc[:, columns(n)] + dot(s_sc[1], flat[0, 1, :, columns(n)], 1, 0)
     for g in SUM_ORDER:
         gather(1, g)
+    ones = jnp.ones((8, USERS), BF16)
+    for k in range(LEVELS):
+        level = slice(k * PAD, (k + 1) * PAD)
+        moved = [dot(ones, s_sc[h, level], 1, 1) - dot(ones, r_sc[h, level], 1, 1) for h in range(2)]
+        vg_ref[k : k + 1] = (moved[0] + moved[1])[0:1]
+    for u in range(4):
+        block_rows = hid[0, u * 16 + xy].astype(F32)
+        mine = lax.broadcasted_iota(jnp.int32, (8, F), 0) == z
+        ph_ref[u : u + 1] = jnp.sum(jnp.where(mine, block_rows, 0.0), axis=0, keepdims=True)
+
     arrived(h_z)
     rest = functools.reduce(jnp.add, [hz[k, 1:2] for k in range(NZ)])
     for k in range(NZ):
@@ -358,48 +387,51 @@
         lambda t: hxy.at[xy], lambda d: hxy.at[xy], hx_s.at[0], hx_r.at[0], hxy.at[0 : NXY - 1]
     )
     start(h_xy)
+    upto = []
+    for b in BATCHES:
+        for g in b:
+            gathered(1, g)
+        upto.append(len(shared))
     arrived(h_xy)
     total = hxy[0]
     for d in range(1, NXY):
         total = total + hxy[d]
     hco[0] = total
     hg_copy = pltpu.make_async_remote_copy(
-        hco.at[0], hco.at[1], co_s.at[LEVELS + 1], co_r.at[LEVELS + 1], device_id=other, device_id_type=MESH
+        hco.at[0], hco.at[1], hc_s.at[0], hc_r.at[0], device_id=other, device_id_type=MESH
     )
     hg_copy.start()
-    for g in SUM_ORDER:
-        gathered(1, g)
-
-    wg_copies = []
-    for k in range(LEVELS):
-        grad = acc_sc[k] - dot(r_sc[k * PAD : (k + 1) * PAD], flat[1], 1, 0)
-        own_sc[k] = grad.astype(BF16)
-        copy = pltpu.make_async_remote_copy(
-            own_sc.at[k], oth_sc.at[k], co_s.at[k], co_r.at[k], device_id=other, device_id_type=MESH
-        )
-        copy.start()
-        wg_copies.append(copy)
-    for copy in (hg_copy, vg_copy, *wg_copies):
-        copy.wait_recv()
+    for b, last in zip(BATCHES, upto):
+        have_shared(last)
+        users = batch_users(b)
+        for n in range(F // 256):
+            moved = dot(r_sc[0, :, users], flat[1, 0, users, columns(n)], 1, 0) + dot(
+                r_sc[1, :, users], flat[1, 1, users, columns(n)], 1, 0
+            )
+            total = acc_sc[:, columns(n)] - moved
+            if b != BATCHES[-1]:
+                acc_sc[:, columns(n)] = total
+                continue
+            for k in range(LEVELS):
+                wg_ref[k, :, columns(n)] = total[k * PAD : k * PAD + MOV]
+    hg_copy.wait_recv()
     for copies in started:
         sent(copies)
-    for copy in (*wg_copies, hg_copy, vg_copy):
+    for copy in (hg_copy, *shared):
         copy.wait_send()
 
 
-def finish(own_ref, oth_ref, vco_ref, hco_ref, ph_ref, wg_out, vg_out, hg_out, ph_out, wg, vg, hg, sem):
-    copies = []
-    for i, (src, dst) in enumerate(((ph_ref, ph_out), (vg, vg_out), (hg, hg_out))):
-        copies.append(pltpu.make_async_copy(src, dst, sem.at[i]))
+def finish(wg_ref, vg_ref, hco_ref, ph_ref, wg_out, vg_out, hg_out, ph_out, vg, hg, sem):
+    copies = [
+        pltpu.make_async_copy(src, dst, sem.at[i])
+        for i, (src, dst) in enumerate(((wg_ref, wg_out), (ph_ref, ph_out), (vg, vg_out), (hg, hg_out)))
+    ]
     copies[0].start()
-    vg[...] = (vco_ref[0] + vco_ref[1])[0:LEVELS, 0:MOV]
     copies[1].start()
+    vg[...] = vg_ref[0:LEVELS, 0:MOV]
+    copies[2].start()
     hg[...] = hco_ref[0] + hco_ref[1]
-    copies[2].start()
-    for k in range(LEVELS):
-        wg[k] = own_ref[k, 0:MOV].astype(F32) + oth_ref[k, 0:MOV].astype(F32)
-        copies.append(pltpu.make_async_copy(wg.at[k], wg_out.at[k], sem.at[3 + k]))
-        copies[-1].start()
+    copies[3].start()
     for copy in copies:
         copy.wait()
 
@@ -412,14 +444,13 @@
     parts = pl.pallas_call(
         kernel,
         out_shape=(
-            shape((LEVELS, PAD, F), BF16),
-            shape((LEVELS, PAD, F), BF16),
-            shape((2, 8, PAD), F32),
+            shape((LEVELS, MOV, F), F32),
+            shape((8, PAD), F32),
             shape((2, NZ, 1, 128), F32),
             shape((4, F), F32),
         ),
         in_specs=[hbm] * 6,
-        out_specs=(vmem,) * 5,
+        out_specs=(vmem,) * 4,
         scratch_shapes=[
             pltpu.VMEM((4, 128), jnp.int32), pltpu.VMEM((4, 128), jnp.int32), pltpu.VMEM((4, 128), jnp.int32),
             pltpu.VMEM((LEVELS, MOV, F), BF16), pltpu.VMEM((LEVELS, MOV), F32), pltpu.VMEM((NZ, 1, 128), F32),
@@ -431,21 +462,21 @@
             pltpu.VMEM((NZ, NXY, 1, 128), F32),
             pltpu.VMEM((NZ, NXY, 1, 128), F32),
             pltpu.VMEM((NXY, NZ, 1, 128), F32),
-            pltpu.VMEM((COLS, USERS), BF16),
-            pltpu.VMEM((COLS, USERS), BF16),
+            pltpu.VMEM((2, COLS, USERS), BF16),
+            pltpu.VMEM((2, COLS, USERS), BF16),
             pltpu.VMEM((COLS, WIDEST), F32),
             pltpu.VMEM((2, BLOCKS, 8, F), BF16),
             pltpu.VMEM((2, BLOCKS, 8, F), BF16),
             pltpu.VMEM((2, len(GROUPS), NXY, MOST // 128, 8, 128), BF16),
             pltpu.VMEM((2, len(GROUPS), NXY, MOST // 128, 8, 128), BF16),
             pltpu.VMEM((2, BLOCKS, 8, F), BF16),
-            pltpu.VMEM((2, USERS, F), BF16),
+            pltpu.VMEM((2, 2, USERS, F), BF16),
             pltpu.VMEM((len(GROUPS), MOST // 128, 8, 128), F32),
-            pltpu.VMEM((LEVELS, PAD, F), F32),
+            pltpu.VMEM((COLS, F), F32),
             pltpu.VMEM((NZ, 2, 128), F32),
             pltpu.VMEM((NXY, NZ, 1, 128), F32),
             *[dma((1,))] * 4, *[dma((4, len(GROUPS)))] * 4, *[dma((1,))] * 4,
-            dma((LEVELS + 2,)), dma((LEVELS + 2,)),
+            dma((1,)), dma((1,)), dma((2 * len(BATCHES) + 2 * len(GROUPS),)), dma((2 * len(BATCHES) + 2 * len(GROUPS),)),
         ],
         compiler_params=pltpu.CompilerParams(
             collective_id=0, has_side_effects=True, vmem_limit_bytes=36 << 20
@@ -457,10 +488,10 @@
     wg, vg, hg, ph = pl.pallas_call(
         finish,
         out_shape=(shape((LEVELS, MOV, F), F32), shape((LEVELS, MOV), F32), shape((NZ, 1, 128), F32), shape((4, F), F32)),
-        in_specs=[vmem] * 5,
+        in_specs=[vmem] * 4,
         out_specs=(hbm,) * 4,
         scratch_shapes=[
-            pltpu.VMEM((LEVELS, MOV, F), F32), pltpu.VMEM((LEVELS, MOV), F32), pltpu.VMEM((NZ, 1, 128), F32), dma((8,)),
+            pltpu.VMEM((LEVELS, MOV), F32), pltpu.VMEM((NZ, 1, 128), F32), dma((4,)),
         ],
         compiler_params=pltpu.CompilerParams(vmem_limit_bytes=8 << 20),
     )(*parts)

time: 83 us -> 81.1 us (0.977)
  Pallas kernels: 82.3 us -> 80.4 us
    pallas_call x1, Pallas kernels: 80.5 us -> 78.7 us  [on_device(): pl.pallas_call(kernel, out_shape=(shape((LEVELS, MOV, F), F32), shape((8,...]
where the time goes in v4:
time: 81.1 us; the launch traced here: 81 us
  Pallas kernels  80.4 us (99%)
    pallas_call x1, Pallas kernels, on_device(): pl.pallas_call(kernel, out_shape=(shape((LEVELS, MOV, F), F32), shape((8,...  78.7 us
    pallas_call x1, Pallas kernels, on_device(): pl.pallas_call(finish, out_shape=(shape((LEVELS, MOV, F), F32), shape((LE...  1.64 us

profile of v4, /device:TPU:1, one launch (start us, length us, event | category | flops | bytes accessed | tf_op | source)
XLA Modules:
  0.0 81.0 jit_solution(2817305080084215620)
XLA Ops:
  0.6 78.7 %shard_map.93 = (f32[5,140,1024]{2,1,0:T(8,128)S(1)}, f32[8,144]{1,0:T(8,128)S(1)}, f32[2,8,1,128]{3,2,1,0:T(1,128)S(1)}, f32[4,1024]{1,0:T(4,128)S(1)}) custom-call(s32[4,128]{1,0:T(4,128)} %ids_hbm.1, s32[4,128]{1,0:T(4,128)} %rat_hbm.1, s32[4,128]{1,0:T(4,128)} %val_hbm.1, bf16[5,140,1024]{2,1,0:T(8,128)(2,1)} %w_hbm.1, f32[5,140]{1,0:T(8,128)} %vb_hbm.1, ...), custom_call_target="tpu_custom_call" | custom-call | tf_op jit(solution)/shard_map/pallas_call | solution.py:444
  79.4 1.6 %shard_map.94 = (f32[5,140,1024]{2,1,0:T(8,128)}, f32[5,140]{1,0:T(8,128)}, f32[8,1,128]{2,1,0:T(1,128)}, f32[4,1024]{1,0:T(4,128)}) custom-call(f32[5,140,1024]{2,1,0:T(8,128)S(1)} %get-tuple-element.12.wg_ref, f32[8,144]{1,0:T(8,128)S(1)} %get-tuple-element.13.vg_ref, f32[2,8,1,128]{3,2,1,0:T(1,128)S(1)} %get-tuple-element.14.hco_ref, ...), custom_call_target="tpu_custom_call" | custom-call | tf_op jit(solution)/shard_map/pallas_call | solution.py:488

commit v5 on v4

--- a/solution.py
+++ b/solution.py
@@ -297,7 +297,7 @@
         flat[c, core, users_of(g)] = rows.reshape(rows.shape[0] * 8, F).astype(BF16)
         share(flat.at[c, core, users_of(g)], flat.at[c, 1 - core, users_of(g)])
 
-    for b in BATCHES:
+    for b in ((0,), (1,), (2, 3)):
         for u in range(batch_users(b).start // 128, batch_users(b).stop // 128):
             picks = [chosen[u * 16 + k : u * 16 + k + 1] for k in range(CAP)]
 
@@ -476,7 +476,7 @@
             pltpu.VMEM((NZ, 2, 128), F32),
             pltpu.VMEM((NXY, NZ, 1, 128), F32),
             *[dma((1,))] * 4, *[dma((4, len(GROUPS)))] * 4, *[dma((1,))] * 4,
-            dma((1,)), dma((1,)), dma((2 * len(BATCHES) + 2 * len(GROUPS),)), dma((2 * len(BATCHES) + 2 * len(GROUPS),)),
+            dma((1,)), dma((1,)), dma((4 * len(GROUPS),)), dma((4 * len(GROUPS),)),
         ],
         compiler_params=pltpu.CompilerParams(
             collective_id=0, has_side_effects=True, vmem_limit_bytes=36 << 20

time: 81.1 us -> 80.9 us (level)
  no operation moved by 1% of the time
where the time goes in v5:
time: 80.9 us; the launch traced here: 80.8 us
  Pallas kernels  80.1 us (99%)
    pallas_call x1, Pallas kernels, on_device(): pl.pallas_call(kernel, out_shape=(shape((LEVELS, MOV, F), F32), shape((8,...  78.5 us
    pallas_call x1, Pallas kernels, on_device(): pl.pallas_call(finish, out_shape=(shape((LEVELS, MOV, F), F32), shape((LE...  1.64 us

profile of v5, /device:TPU:1, one launch (start us, length us, event | category | flops | bytes accessed | tf_op | source)
XLA Modules:
  0.0 80.8 jit_solution(10442995150322383581)
XLA Ops:
  0.6 78.5 %shard_map.93 = (f32[5,140,1024]{2,1,0:T(8,128)S(1)}, f32[8,144]{1,0:T(8,128)S(1)}, f32[2,8,1,128]{3,2,1,0:T(1,128)S(1)}, f32[4,1024]{1,0:T(4,128)S(1)}) custom-call(s32[4,128]{1,0:T(4,128)} %ids_hbm.1, s32[4,128]{1,0:T(4,128)} %rat_hbm.1, s32[4,128]{1,0:T(4,128)} %val_hbm.1, bf16[5,140,1024]{2,1,0:T(8,128)(2,1)} %w_hbm.1, f32[5,140]{1,0:T(8,128)} %vb_hbm.1, ...), custom_call_target="tpu_custom_call" | custom-call | tf_op jit(solution)/shard_map/pallas_call | solution.py:444
  79.1 1.6 %shard_map.94 = (f32[5,140,1024]{2,1,0:T(8,128)}, f32[5,140]{1,0:T(8,128)}, f32[8,1,128]{2,1,0:T(1,128)}, f32[4,1024]{1,0:T(4,128)}) custom-call(f32[5,140,1024]{2,1,0:T(8,128)S(1)} %get-tuple-element.12.wg_ref, f32[8,144]{1,0:T(8,128)S(1)} %get-tuple-element.13.vg_ref, f32[2,8,1,128]{3,2,1,0:T(1,128)S(1)} %get-tuple-element.14.hco_ref, ...), custom_call_target="tpu_custom_call" | custom-call | tf_op jit(solution)/shard_map/pallas_call | solution.py:488

commit v6 on v5

--- a/solution.py
+++ b/solution.py
@@ -19,7 +19,7 @@
 BLOCKS = USERS // 8
 GROUPS = ((0, 128, True), (128, 128, False), (256, 128, False), (384, 128, False))
 SUM_ORDER = (0, 1, 2, 3)
-PIPE = ((0, 1), (0, 0), (0, 2), (1, 1), (0, 3), (1, 0), (1, 2), (2, 1), (1, 3), (2, 0), (2, 2), (2, 3))
+PIPE = ((0, 1), (0, 0), (0, 2), (0, 3), (1, 1), (1, 0), (1, 2), (2, 1), (1, 3), (2, 0), (2, 2), (2, 3))
 BATCHES = ((0, 1), (2, 3))
 MOST = max(n for _, n, _ in GROUPS)
 WIDEST = 256

time: 80.9 us -> 81.3 us (level)
  no operation moved by 1% of the time
where the time goes in v6:
time: 81.3 us
  Pallas kernels  80.6 us (99%)
    pallas_call x1, Pallas kernels, on_device(): pl.pallas_call(kernel, out_shape=(shape((LEVELS, MOV, F), F32), shape((8,...  79 us
    pallas_call x1, Pallas kernels, on_device(): pl.pallas_call(finish, out_shape=(shape((LEVELS, MOV, F), F32), shape((LE...  1.64 us

profile of v6, /device:TPU:1, one launch (start us, length us, event | category | flops | bytes accessed | tf_op | source)
XLA Modules:
  0.0 81.3 jit_solution(15606925351919943303)
XLA Ops:
  0.6 79.0 %shard_map.93 = (f32[5,140,1024]{2,1,0:T(8,128)S(1)}, f32[8,144]{1,0:T(8,128)S(1)}, f32[2,8,1,128]{3,2,1,0:T(1,128)S(1)}, f32[4,1024]{1,0:T(4,128)S(1)}) custom-call(s32[4,128]{1,0:T(4,128)} %ids_hbm.1, s32[4,128]{1,0:T(4,128)} %rat_hbm.1, s32[4,128]{1,0:T(4,128)} %val_hbm.1, bf16[5,140,1024]{2,1,0:T(8,128)(2,1)} %w_hbm.1, f32[5,140]{1,0:T(8,128)} %vb_hbm.1, ...), custom_call_target="tpu_custom_call" | custom-call | tf_op jit(solution)/shard_map/pallas_call | solution.py:444
  79.6 1.6 %shard_map.94 = (f32[5,140,1024]{2,1,0:T(8,128)}, f32[5,140]{1,0:T(8,128)}, f32[8,1,128]{2,1,0:T(1,128)}, f32[4,1024]{1,0:T(4,128)}) custom-call(f32[5,140,1024]{2,1,0:T(8,128)S(1)} %get-tuple-element.12.wg_ref, f32[8,144]{1,0:T(8,128)S(1)} %get-tuple-element.13.vg_ref, f32[2,8,1,128]{3,2,1,0:T(1,128)S(1)} %get-tuple-element.14.hco_ref, ...), custom_call_target="tpu_custom_call" | custom-call | tf_op jit(solution)/shard_map/pallas_call | solution.py:488
